TPU v7x, 1024 devices: a whole 8x8x8 slice. The times are simulated.
1024 devices in a mesh: row: 64 (over x, y), col: 16 (over z, core).
Axes of the slice: x: 8, y: 8, z: 8, core: 2. Of those that a mesh axis runs over, the one named last changes fastest.
Arguments:
- x_tiles: bfloat16 [1024, 8, 256, 256], P(('row', 'col')), as said below
- columns: int32 [1024, 8], P(('row', 'col')), may hold values from 0 to 1023, as said below
- branch: int32 [64, 2], P('row'), may hold values from 0 to 1
Outputs:
- purified: float32 [1024, 8, 256, 256], P(('row', 'col'))
- occupation: float32 [64], P('row')
Inputs may be any that keep to these rules, and one draw needn't show every extreme that they name: `columns`: block rows form fragments of 16 consecutive rows, each with two halves of 8 rows. Slot 0 of a block row is the row itself; its other slots hold, in ascending order, every row of the other half of its fragment but one, so that the pattern is symmetric and no two rows of one half are coupled. `x_tiles`: every tile of the pattern is the transpose of its mirror tile, and diagonal tiles are symmetric.
All inputs are finite; a program needn't handle non-finite values.
Results may differ from a plain program's by a relative error of at most 0.0028.
Values may be sent and summed in bfloat16 or wider, within the bound.
No kernel may reach another device: no remote copies, remote signals or barrier semaphores. Data moves between devices by JAX's collectives and lax.ppermute only.
A program may use at most 32 MiB of HBM per device.

v0:
```python
import jax
import jax.numpy as jnp
from jax import lax
from jax.sharding import PartitionSpec as P


def gather_partner_terms(rounded, partner):
    diagonal = rounded[:, 0]
    others = rounded[:, 1:]
    pieces = lax.all_gather(diagonal, "col", axis=0, tiled=True)
    width = pieces.shape[0]
    weights = (partner[:, :, None] == jnp.arange(width, dtype=jnp.int32)).astype(jnp.bfloat16)
    chosen = jnp.einsum(
        "bsm,mjk->bsjk", weights, pieces, preferred_element_type=jnp.float32
    ).astype(jnp.bfloat16)
    product = jnp.einsum("bsij,bskj->bsik", others, chosen, preferred_element_type=jnp.float32)
    return lax.optimization_barrier(product.astype(jnp.bfloat16)).astype(jnp.float32)


def shards(x_tiles, columns, branch):
    rows_dev = x_tiles.shape[0]
    tile_size = x_tiles.shape[2]
    col_count = lax.axis_size("col")
    cluster_rows = rows_dev * col_count
    local_cols = columns % cluster_rows
    partner = local_cols[:, 1:]
    identity = jnp.eye(tile_size, dtype=jnp.float32)
    current = x_tiles.astype(jnp.float32)
    for iteration in range(branch.shape[1]):
        step_sign = (2 * branch[0, iteration] - 1).astype(jnp.float32)
        rounded = current.astype(jnp.bfloat16)
        diagonal_sum = jnp.einsum(
            "btij,btkj->bik", rounded, rounded, preferred_element_type=jnp.float32
        )
        local_term = jnp.einsum(
            "bij,bsjk->bsik", rounded[:, 0], rounded[:, 1:], preferred_element_type=jnp.float32
        )
        partner_term = gather_partner_terms(rounded, partner)
        new_diagonal = current[:, 0] + step_sign * (diagonal_sum - 0.25 * identity)
        new_others = current[:, 1:] + step_sign * (local_term + partner_term)
        current = jnp.concatenate([new_diagonal[:, None], new_others], axis=1)
    trace_sum = jnp.sum(jnp.diagonal(current[:, 0], axis1=1, axis2=2))
    summed = lax.psum(trace_sum, "col")
    occupation = (summed / (cluster_rows * tile_size) + 0.5).reshape(1)
    return (current, occupation)


def solution(mesh):
    placed = (P(("row", "col"), None, None, None), P(("row", "col"), None), P("row", None))
    return jax.shard_map(
        shards,
        mesh=mesh,
        in_specs=placed,
        out_specs=(P(("row", "col"), None, None, None), P("row")),
        check_vma=False,
    )
```

profile of v0, /device:TPU:1, one launch (start us, length us, event | category | flops | bytes accessed | tf_op | source)
XLA Modules:
  0.0 161.7 jit_solution(16049659655894072271)
XLA Ops:
  7.2 0.0 copy-start.2
  7.2 0.0 copy-start.4
  7.2 0.0 all-gather.5.cloned.1.call-start
  7.2 1.6 %slice.32 = bf16[1,1,256,256]{3,2,1,0:T(8,128)(2,1)} slice(bf16[1,8,256,256]{3,2,1,0:T(8,128)(2,1)} %param.3), slice={[0:1], [0:1], [0:256], [0:256]} | slice | bytes 262144 | tf_op jit(solution)/shard_map/slice | solution.py:36
  8.9 0.0 all-gather.5.cloned.1.call-update
  8.9 0.0 all-gather.7.cloned.1.call-start
  8.9 1.4 convert_element_type.59
  10.4 0.0 copy-done.4
  10.4 0.0 copy-start
  10.4 0.0 copy-start.5
  10.4 0.6 fusion.42
  11.6 0.1 copy-done
  11.7 0.0 copy-done.2
  11.7 1.1 fusion.43
  12.8 0.0 all-gather.7.cloned.1.call-update
  13.6 0.1 slice_bitcast_fusion.1
  13.6 56.5 %all-gather.5.cloned.1.call-done = bf16[16,1,256,256]{3,2,1,0:T(8,128)(2,1)} async-done(((bf16[1,1,256,256]{3,2,1,0:T(8,128)(2,1)}), bf16[16,1,256,256]{3,2,1,0:T(8,128)(2,1)}) %all-gather.5.cloned.1.call-update) | async-done | bytes 2097168 | tf_op jit(solution)/shard_map/all_gather | solution.py:10
  70.1 2.8 %fusion.11 = bf16[7,256,256]{2,0,1:T(8,128)(2,1)S(1)} fusion(bf16[16,1,256,256]{3,2,1,0:T(8,128)(2,1)} %all-gather.5.cloned.1.call-done, s32[7]{0:T(128)S(1)} %slice_bitcast_fusion.1), kind=kOutput, calls=%fused_computation.14 | convolution fusion | flops 15138928 | bytes 3014684 | tf_op jit(solution)/shard_map/bsm,mjk->bsjk/dot_general | solution.py:13
  73.0 0.5 fusion.14
  73.4 1.1 copy-done.1
  74.6 0.4 slice_add_fusion
  75.0 42.4 %all-gather.7.cloned.1.call-done = bf16[4096,256]{1,0:T(8,128)(2,1)} async-done(((bf16[256,256]{1,0:T(8,128)(2,1)}), bf16[4096,256]{1,0:T(8,128)(2,1)}) %all-gather.7.cloned.1.call-update) | async-done | bytes 2097168 | tf_op jit(solution)/shard_map/all_gather | solution.py:10
  117.4 2.8 %fusion.8 = bf16[7,256,256]{2,0,1:T(8,128)(2,1)S(1)} fusion(bf16[16,256,256]{2,1,0:T(8,128)(2,1)} %bitcast.86, s32[7]{0:T(128)S(1)} %slice_bitcast_fusion.1), kind=kOutput, calls=%fused_computation.13 | convolution fusion | flops 15138928 | bytes 3014684 | tf_op jit(solution)/shard_map/bsm,mjk->bsjk/dot_general | solution.py:13
  120.2 0.1 convert_bitcast_fusion
  120.3 0.5 fusion.15
  120.8 0.4 copy-done.3
  121.2 0.5 fusion.21
  121.7 2.3 %gather_fusion = f32[256]{0:T(256)S(1)} fusion(f32[256,256]{1,0:T(8,128)S(1)} %fusion.21, s32[256]{0:T(256)S(1)} %bitcast.84), kind=kCustom, calls=%fused_computation | custom fusion | bytes 4096 | tf_op jit(solution)/shard_map/jit(diagonal)/gather | solution.py:42
  124.1 0.6 reduce
  124.7 1.7 %fusion.6 = f32[1,7,256,256]{3,2,1,0:T(8,128)} fusion(f32[1,7,256,256]{3,2,1,0:T(8,128)S(1)} %slice_add_fusion, bf16[1,7,256,256]{3,2,1,0:T(8,128)(2,1)S(1)} %fusion.15, f32[]{:T(128)} %bitcast.4, bf16[256,256]{1,0:T(8,128)(2,1)S(1)} %copy-done.3), kind=kOutput, calls=%fused_computation.10 | convolution fusion | flops 237174784 | bytes 4718596 | tf_op jit(solution)/shard_map/bij,bsjk->bsik/dot_general | solution.py:35
  126.4 23.8 %psum.7 = f32[]{:T(128)} all-reduce(f32[]{:T(128)} %reduce), channel_id=1, replica_groups=mesh['row'=64,'col'=16] {'col'}, use_global_device_ids=true, to_apply=%region_1.2 | all-reduce | flops 1 | bytes 8 | tf_op jit(solution)/shard_map/psum | solution.py:43
  150.2 3.0 %pad_maximum_fusion = f32[1,8,256,256]{3,2,1,0:T(8,128)} fusion(f32[1,7,256,256]{3,2,1,0:T(8,128)} %fusion.6, f32[1,1,256,256]{3,2,1,0:T(8,128)S(1)} %bitcast.85), kind=kLoop, calls=%fused_computation.1 | loop fusion | flops 524288 | bytes 4194304 | tf_op jit(solution)/shard_map/concatenate | solution.py:41
  (5 shorter events, 0.0 us)
Async XLA Ops:
  7.2 4.5 %copy-start.2 = (bf16[1,8,256,256]{3,2,1,0:T(8,128)(2,1)S(1)}, bf16[1,8,256,256]{3,2,1,0:T(8,128)(2,1)}, u32[]{:S(2)}) copy-start(bf16[1,8,256,256]{3,2,1,0:T(8,128)(2,1)} %param.3) | copy-start | bytes 3145732
  7.2 3.2 %copy-start.4 = (s32[1,2]{1,0:T(1,128)S(1)}, s32[1,2]{1,0:T(1,128)}, u32[]{:S(2)}) copy-start(s32[1,2]{1,0:T(1,128)} %param.5) | copy-start | bytes 28
  7.2 62.9 %all-gather.5.cloned.1.call-start = ((), (), s32[]{:S(2)}) async-start(), calls=%async_computation | async-start | bytes 2228224 | tf_op jit(solution)/shard_map/all_gather | solution.py:10
  8.9 108.5 %all-gather.7.cloned.1.call-start = ((), (), s32[]{:S(2)}) async-start(), calls=%async_computation.1 | async-start | bytes 2228224 | tf_op jit(solution)/shard_map/all_gather | solution.py:10
  10.4 1.3 copy-start
  10.4 3.1 %copy-start.5 = (s32[1,8]{1,0:T(1,128)S(1)}, s32[1,8]{1,0:T(1,128)}, u32[]{:S(2)}) copy-start(s32[1,8]{1,0:T(1,128)} %param.4) | copy-start | bytes 100
  73.0 1.6 copy-start.1
  120.3 0.9 copy-start.3
Sparse Core Ops, SparseCore 0:
  10.7 59.3 all-gather.4
  72.8 44.5 all-gather.6
where the time goes:
time: 163 us; the launch traced here: 162 us
  waiting for transfers between devices  98.9 us (61%)
  blocking collectives  23.8 us (15%)
  between operations  17.2 us (11%)
  matrix products  10.4 us (6%)
  local copies, waits for them, and re-layouts  6.29 us (4%)
  other arithmetic  5.08 us (3%)
    all_gather x2, waiting for transfers between devices, gather_partner_terms(): pieces = lax.all_gather(diagonal, 'col', axis=0, tiled=True)  98.9 us
    psum x1, blocking collectives, shards(): summed = lax.psum(trace_sum, 'col')  23.8 us
    dot_general x2, matrix products, gather_partner_terms(): jnp.einsum('bsm,mjk->bsjk', weights, pieces, preferred_element_type=jnp.f...  5.66 us
  transfers between devices with their start and end apart: 2, of which 2 were waited for; matrix products, arithmetic and copies ran while one was open for 4% of the time, Pallas kernels for 0%

commit v1 on v0

v1 whole, which is shorter than its diff:
```python
import jax
import jax.numpy as jnp
from jax import lax
from jax.experimental import pallas as pl
from jax.experimental.pallas import tpu as pltpu
from jax.sharding import PartitionSpec as P

BF = jnp.bfloat16
F32 = jnp.float32
SIDE_ROWS = 8


def nt(a, b):
    return lax.dot_general(a, b, (((1,), (1,)), ((), ())), preferred_element_type=F32)


def nn(a, b):
    return jnp.dot(a, b, preferred_element_type=F32)


def index_grids(h):
    return (lax.broadcasted_iota(jnp.int32, (h, h), 0), lax.broadcasted_iota(jnp.int32, (h, h), 1))


def quarter_identity(size):
    row, col = index_grids(size)
    return jnp.where(row == col, 0.25, 0.0).astype(F32)


def sign_of(branch_ref, step):
    return (2 * branch_ref[0, step] - 1).astype(F32)


def folded(tile):
    h = tile.shape[0] // 2
    row, col = index_grids(h)
    first, second = tile[:h, :h], tile[h:, h:]
    mixed = jnp.where(row <= col, first, second)
    second_diag = jnp.sum(jnp.where(row == col, second, 0.0), axis=0, keepdims=True)
    return mixed, tile[:h, h:], second_diag


def unfolded(mixed, corner, second_diag, grids):
    row, col = grids
    low = jnp.where(row > col, mixed, 0.0)
    zero = jnp.zeros_like(low)
    stack = lambda a, b, c, d: jnp.concatenate(
        [jnp.concatenate([a, b], axis=1), jnp.concatenate([c, d], axis=1)], axis=0
    ).astype(BF)
    straight = stack(jnp.where(row <= col, mixed, 0.0), corner, zero, jnp.where(row == col, second_diag, low))
    flipped = stack(jnp.where(row < col, mixed, 0.0), corner, zero, low)
    return straight, flipped


def partner_product(tile, index, gathered_ref, side_ref, rows_ref, grids, diag_row, tail_rows):
    h = gathered_ref.shape[2]
    rows_ref[: gathered_ref.shape[1]] = gathered_ref[index].astype(F32)
    side = side_ref[index].astype(F32)
    for k, where in enumerate(tail_rows):
        at = 2 * h - len(tail_rows) + k
        rows_ref[at : at + 1] = side[where : where + 1]
    straight, flipped = unfolded(rows_ref[:h], rows_ref[h:], side[diag_row : diag_row + 1], grids)
    return (nn(tile, straight) + nt(tile, flipped)).astype(BF).astype(F32)


def first_kernel(branch_ref, x_hbm, sent0_ref, side_ref, sent1_ref, diag_ref, x_ref, sems):
    tiles, size = x_ref.shape[:2]
    h = size // 2
    loads = [pltpu.make_async_copy(x_hbm.at[s], x_ref.at[s], sems.at[s]) for s in range(tiles)]
    for load in loads:
        load.start()
    sign = sign_of(branch_ref, 0)
    loads[0].wait()
    x0 = x_ref[0]
    old = x0.astype(F32)
    mixed0, corner0, diag0 = folded(old)
    sent0_ref[0, :h] = mixed0.astype(BF)
    sent0_ref[0, h:] = corner0[: h - 1].astype(BF)
    total = nt(x0, x0)
    for slot in range(1, tiles):
        loads[slot].wait()
        total += nt(x_ref[slot], x_ref[slot])
    new = old + sign * (total - quarter_identity(size))
    diag_ref[...] = new
    mixed1, corner1, diag1 = folded(new)
    sent1_ref[:h] = mixed1.astype(BF)
    sent1_ref[h:] = corner1[: h - 1].astype(BF)
    at = lax.broadcasted_iota(jnp.int32, (SIDE_ROWS, h), 0)
    side = jnp.zeros((SIDE_ROWS, h), F32)
    for k, line in enumerate((diag0, corner0[h - 1 :], diag1, corner1[h - 2 : h - 1], corner1[h - 1 :])):
        side = jnp.where(at == k, line, side)
    for slot in range(side_ref.shape[0]):
        side_ref[slot] = side.astype(BF)


def second_kernel(
    cluster, branch_ref, cols_ref, x_hbm, diag_ref, held_ref, gathered_ref, side_ref,
    new_hbm, sent_ref, x_ref, new_ref, rows_ref, load_sems, store_sems,
):
    tiles, size = x_ref.shape[:2]
    h = size // 2
    loads = [pltpu.make_async_copy(x_hbm.at[s], x_ref.at[s], load_sems.at[s]) for s in range(tiles)]
    stores = [pltpu.make_async_copy(new_ref.at[s], new_hbm.at[s], store_sems.at[s]) for s in range(tiles - 1)]
    for load in loads:
        load.start()
    sign, next_sign = sign_of(branch_ref, 0), sign_of(branch_ref, 1)
    grids = index_grids(h)
    diag = diag_ref[...]
    rounded = diag.astype(BF).astype(F32)
    squares = rounded * rounded
    loads[0].wait()
    x0 = x_ref[0]
    for slot in range(1, tiles):
        loads[slot].wait()
        tile = x_ref[slot]
        index = lax.rem(cols_ref[0, slot], cluster)
        partner = partner_product(tile, index, gathered_ref, side_ref, rows_ref, grids, 0, (1,))
        new = tile.astype(F32) + sign * (nn(x0, tile) + partner)
        new_ref[slot - 1] = new
        stores[slot - 1].start()
        rounded = new.astype(BF).astype(F32)
        squares += rounded * rounded
    row, col = index_grids(size)
    trace = jnp.sum(jnp.where(row == col, diag - 0.25 * next_sign, 0.0) + next_sign * squares)
    lane = lax.broadcasted_iota(jnp.int32, (1, h), 1)
    left = jnp.full((1, h), trace, F32)
    line = jnp.zeros((1, h), F32)
    for k in range(3):
        piece = left.astype(BF).astype(F32)
        line = jnp.where(lane == k, piece, line)
        left = left - piece
    last = sent_ref.shape[1] - 1
    at = lax.broadcasted_iota(jnp.int32, (last + 1, h), 0)
    sent_ref[0] = jnp.where(at == last, line, held_ref[...].astype(F32)).astype(BF)
    for store in stores:
        store.wait()


def third_kernel(
    cluster, branch_ref, cols_ref, diag_ref, new_hbm, gathered_ref, side_ref,
    out_hbm, occupation_ref, new_ref, out_ref, rows_ref, load_sems, store_sems,
):
    tiles, size = out_ref.shape[:2]
    loads = [pltpu.make_async_copy(new_hbm.at[s], new_ref.at[s], load_sems.at[s]) for s in range(tiles - 1)]
    stores = [pltpu.make_async_copy(out_ref.at[s], out_hbm.at[s], store_sems.at[s]) for s in range(tiles)]
    for load in loads:
        load.start()
    sign = sign_of(branch_ref, 1)
    grids = index_grids(size // 2)
    last = gathered_ref.shape[1] - 1
    lines = jnp.zeros((1, size // 2), F32)
    for member in range(cluster):
        lines += gathered_ref[member].astype(F32)[last:]
    occupation_ref[0] = jnp.sum(lines) / (cluster * size) + 0.5
    diag = diag_ref[...]
    r0 = diag.astype(BF)
    total = nt(r0, r0)
    for slot in range(1, tiles):
        loads[slot - 1].wait()
        new = new_ref[slot - 1]
        r = new.astype(BF)
        total += nt(r, r)
        index = lax.rem(cols_ref[0, slot], cluster)
        partner = partner_product(r, index, gathered_ref, side_ref, rows_ref, grids, 2, (3, 4))
        out_ref[slot] = new + sign * (nn(r0, r) + partner)
        stores[slot].start()
    out_ref[0] = diag + sign * (total - quarter_identity(size))
    stores[0].start()
    for store in stores:
        store.wait()


S, V, A = (pl.BlockSpec(memory_space=m) for m in (pltpu.SMEM, pltpu.VMEM, pl.ANY))


def call(kernel, ins, outs, scratch, args, name):
    return pl.pallas_call(
        kernel,
        out_shape=[jax.ShapeDtypeStruct(shape, dtype) for shape, dtype, _ in outs],
        in_specs=list(ins),
        out_specs=[spec for _, _, spec in outs],
        scratch_shapes=scratch,
        compiler_params=pltpu.CompilerParams(vmem_limit_bytes=24 * 1024 * 1024),
        name=name,
    )(*args)


def shards(x_tiles, columns, branch):
    tiles, size = x_tiles.shape[1], x_tiles.shape[2]
    h = size // 2
    cluster = x_tiles.shape[0] * lax.axis_size("col")
    x = x_tiles.reshape(tiles, size, size)
    sems = pltpu.SemaphoreType.DMA((tiles,))
    many = pltpu.VMEM((tiles, size, size), BF)
    fewer = (tiles - 1, size, size)

    sent0, side, held, diag = call(
        first_kernel,
        (S, A),
        [((1, size - 1, h), BF, V), ((cluster, SIDE_ROWS, h), BF, V), ((size - 1, h), BF, V), ((size, size), F32, V)],
        [many, sems],
        (branch, x),
        "first",
    )
    sides = lax.all_to_all(side, "col", 0, 0, tiled=True)
    gathered0 = lax.all_gather(sent0, "col", axis=0, tiled=True)
    new, sent1 = call(
        lambda *refs: second_kernel(cluster, *refs),
        (S, S, A, V, V, V, V),
        [(fewer, F32, A), ((1, size - 1, h), BF, V)],
        [many, pltpu.VMEM(fewer, F32), pltpu.VMEM((size, h), F32), sems, sems],
        (branch, columns, x, diag, held, gathered0, sides),
        "second",
    )
    gathered1 = lax.all_gather(sent1, "col", axis=0, tiled=True)
    out, occupation = call(
        lambda *refs: third_kernel(cluster, *refs),
        (S, S, V, A, V, V),
        [((tiles, size, size), F32, A), ((1,), F32, S)],
        [pltpu.VMEM(fewer, F32), pltpu.VMEM((tiles, size, size), F32), pltpu.VMEM((size, h), F32), sems, sems],
        (branch, columns, diag, new, gathered1, sides),
        "third",
    )
    return out.reshape(x_tiles.shape), occupation


def solution(mesh):
    placed = (P(("row", "col"), None, None, None), P(("row", "col"), None), P("row", None))
    return jax.shard_map(
        shards,
        mesh=mesh,
        in_specs=placed,
        out_specs=(P(("row", "col"), None, None, None), P("row")),
        check_vma=False,
    )
```

time: 163 us -> 73.2 us (0.45)
  waiting for transfers between devices: 98.9 us -> 0.01 us
  starting transfers between devices: 0.08 us -> 18.2 us
  between operations: 17.2 us -> 0.69 us
  blocking collectives: 23.8 us -> 38.4 us
  Pallas kernels: 0 us -> 13.8 us
  matrix products: 10.4 us -> 0 us
  other arithmetic: 5.08 us -> 0 us
  local copies, waits for them, and re-layouts: 6.29 us -> 1.9 us
    all_gather x2 -> x0, waiting for transfers between devices: 98.9 us -> none  [gather_partner_terms(): pieces = lax.all_gather(diagonal, 'col', axis=0, tiled=True)]
    all_gather x0 -> x2, blocking collectives: none -> 38.4 us  [the longest x1 20.1 us: shards(): gathered0 = lax.all_gather(sent0, 'col', axis=0, tiled=True)]
    psum x1 -> x0, blocking collectives: 23.8 us -> none  [shards(): summed = lax.psum(trace_sum, 'col')]
    all_to_all x0 -> x1, starting transfers between devices: none -> 18.2 us  [shards(): sides = lax.all_to_all(side, 'col', 0, 0, tiled=True)]
    pallas_call x0 -> x3, Pallas kernels: none -> 13.8 us  [call(): pl.pallas_call(kernel, out_shape=[jax.ShapeDtypeStruct(shape, dtype) for...]
    dot_general x8 -> x0, matrix products: 10.4 us -> none  [the longest x2 5.66 us: gather_partner_terms(): jnp.einsum('bsm,mjk->bsjk', weights, pieces, preferred_element_type=jnp.f...]
    concatenate x3 -> x0, other arithmetic: 3.06 us -> none  [the longest x2 3.05 us: shards(): current = jnp.concatenate([new_diagonal[:, None], new_others], axis=1)]
    gather x1 -> x0, local copies, waits for them, and re-layouts: 2.34 us -> none  [shards(): trace_sum = jnp.sum(jnp.diagonal(current[:, 0], axis1=1, axis2=2))]
  transfers between devices with their start and end apart: 2 -> 1, of which waited for: 2 -> 0; matrix products, arithmetic and copies ran while one was open for 4% -> 0% of each run, Pallas kernels for 0% -> 0%
where the time goes in v1:
time: 73.2 us; the launch traced here: 73 us
  blocking collectives  38.4 us (52%)
  starting transfers between devices  18.2 us (25%)
  Pallas kernels  13.8 us (19%)
  local copies, waits for them, and re-layouts  1.9 us (3%)
    all_gather x1, blocking collectives, shards(): gathered0 = lax.all_gather(sent0, 'col', axis=0, tiled=True)  20.1 us
    all_gather x1, blocking collectives, shards(): gathered1 = lax.all_gather(sent1, 'col', axis=0, tiled=True)  18.3 us
    all_to_all x1, starting transfers between devices, shards(): sides = lax.all_to_all(side, 'col', 0, 0, tiled=True)  18.2 us
    pallas_call x3, Pallas kernels, call(): pl.pallas_call(kernel, out_shape=[jax.ShapeDtypeStruct(shape, dtype) for...  13.8 us
    unnamed x10, local copies, waits for them, and re-layouts  1.9 us
  transfers between devices with their start and end apart: 1, of which 0 were waited for; matrix products, arithmetic and copies ran while one was open for 0% of the time, Pallas kernels for 0%

profile of v1, /device:TPU:1, one launch (start us, length us, event | category | flops | bytes accessed | tf_op | source)
XLA Modules:
  0.0 73.0 jit_solution(1440263274000804722)
XLA Ops:
  0.6 0.0 copy-start.3
  0.6 0.0 copy-start.4
  0.6 0.0 copy-start
  0.7 1.2 %copy-done = bf16[1,8,256,256]{3,2,1,0:T(8,128)(2,1)S(1)} copy-done((bf16[1,8,256,256]{3,2,1,0:T(8,128)(2,1)S(1)}, bf16[1,8,256,256]{3,2,1,0:T(8,128)(2,1)}, u32[]{:S(2)}) %copy-start) | copy-done | bytes 1048600
  1.9 0.0 copy-start.2
  1.9 0.7 copy-done.2
  2.5 0.0 copy-start.1
  2.5 3.9 %first.1 = (bf16[1,255,128]{2,1,0:T(8,128)(2,1)S(1)}, bf16[16,8,128]{2,1,0:T(8,128)(2,1)}, bf16[255,128]{1,0:T(8,128)(2,1)S(1)}, f32[256,256]{1,0:T(8,128)S(1)}) custom-call(s32[1,2]{1,0:T(1,128)S(1)} %copy-done.2, bf16[8,256,256]{2,1,0:T(8,128)(2,1)S(1)} %bitcast.2), custom_call_target="tpu_custom_call" | custom-call | tf_op jit(solution)/shard_map/first/pallas_call | solution.py:177
  6.4 18.2 %all-to-all-start = ((bf16[16,8,128]{2,1,0:T(8,128)(2,1)}), bf16[16,8,128]{2,1,0:T(8,128)(2,1)S(1)}, u32[]{:S(2)}, u32[]{:S(2)}) async-start(bf16[16,8,128]{2,1,0:T(8,128)(2,1)} %get-tuple-element.13), calls=%async_computation | async-start | bytes 65536 | tf_op jit(solution)/shard_map/all_to_all | solution.py:205
  24.6 20.1 %all_gather.6.refs_5_ = bf16[16,255,128]{2,1,0:T(8,128)(2,1)S(1)} all-gather(bf16[1,255,128]{2,1,0:T(8,128)(2,1)S(1)} %get-tuple-element.12), channel_id=1, replica_groups=mesh['row'=64,'col'=16] {'col'}, dimensions={0}, use_global_device_ids=true | all-gather | bytes 1109760 | tf_op jit(solution)/shard_map/all_gather | solution.py:206
  44.7 0.0 all-to-all-done.refs_6_.refs_5_
  44.7 0.0 copy-done.3
  44.7 0.0 copy-done.4
  44.7 0.0 copy-done.1
  44.7 5.1 %second.1 = (f32[7,256,256]{2,1,0:T(8,128)S(1)}, bf16[1,255,128]{2,1,0:T(8,128)(2,1)S(1)}) custom-call(s32[1,2]{1,0:T(1,128)S(1)} %copy-done.3, s32[1,8]{1,0:T(1,128)S(1)} %copy-done.4, bf16[8,256,256]{2,1,0:T(8,128)(2,1)S(1)} %bitcast.3, f32[256,256]{1,0:T(8,128)S(1)} %get-tuple-element.10.refs_3_.refs_2_, bf16[255,128]{1,0:T(8,128)(2,1)S(1)} %get-tuple-element.11.refs_4_, ...), custom_call_target="tpu_custom_call" | custom-call | tf_op jit(solution)/shard_map/second/pallas_call | solution.py:177
  49.8 18.3 %all_gather.7.refs_4_ = bf16[16,255,128]{2,1,0:T(8,128)(2,1)S(1)} all-gather(bf16[1,255,128]{2,1,0:T(8,128)(2,1)S(1)} %get-tuple-element.15), channel_id=1, replica_groups=mesh['row'=64,'col'=16] {'col'}, dimensions={0}, use_global_device_ids=true | all-gather | bytes 1109760 | tf_op jit(solution)/shard_map/all_gather | solution.py:215
  68.2 4.8 %third.1 = (f32[8,256,256]{2,1,0:T(8,128)}, f32[1]{0:T(128)}) custom-call(s32[1,2]{1,0:T(1,128)S(1)} %copy-done.3, s32[1,8]{1,0:T(1,128)S(1)} %copy-done.4, f32[256,256]{1,0:T(8,128)S(1)} %get-tuple-element.10.refs_3_.refs_2_, f32[7,256,256]{2,1,0:T(8,128)S(1)} %get-tuple-element.14.refs_3_, bf16[16,255,128]{2,1,0:T(8,128)(2,1)S(1)} %all_gather.7.refs_4_, ...), custom_call_target="tpu_custom_call" | custom-call | tf_op jit(solution)/shard_map/third/pallas_call | solution.py:177
Async XLA Ops:
  0.6 44.1 %copy-start.3 = (s32[1,2]{1,0:T(1,128)S(1)}, s32[1,2]{1,0:T(1,128)}, u32[]{:S(2)}) copy-start(s32[1,2]{1,0:T(1,128)} %refs_0_.3) | copy-start | bytes 28
  0.6 44.1 %copy-start.4 = (s32[1,8]{1,0:T(1,128)S(1)}, s32[1,8]{1,0:T(1,128)}, u32[]{:S(2)}) copy-start(s32[1,8]{1,0:T(1,128)} %refs_1_.3) | copy-start | bytes 100
  0.6 1.2 %copy-start = (bf16[1,8,256,256]{3,2,1,0:T(8,128)(2,1)S(1)}, bf16[1,8,256,256]{3,2,1,0:T(8,128)(2,1)}, u32[]{:S(2)}) copy-start(bf16[1,8,256,256]{3,2,1,0:T(8,128)(2,1)} %param.3) | copy-start | bytes 3145732
  1.9 0.7 copy-start.2
  2.5 42.2 %copy-start.1 = (bf16[1,8,256,256]{3,2,1,0:T(8,128)(2,1)S(1)}, bf16[1,8,256,256]{3,2,1,0:T(8,128)(2,1)}, u32[]{:S(2)}) copy-start(bf16[1,8,256,256]{3,2,1,0:T(8,128)(2,1)} %param.3) | copy-start | bytes 3145732
  6.4 38.3 %all-to-all-start = ((bf16[16,8,128]{2,1,0:T(8,128)(2,1)}), bf16[16,8,128]{2,1,0:T(8,128)(2,1)S(1)}, u32[]{:S(2)}, u32[]{:S(2)}) async-start(bf16[16,8,128]{2,1,0:T(8,128)(2,1)} %get-tuple-element.13), calls=%async_computation | async-start | bytes 65536 | tf_op jit(solution)/shard_map/all_to_all | solution.py:205

commit v2 on v1

v2 whole, which is shorter than its diff:
```python
import jax
import jax.numpy as jnp
from jax import lax
from jax.experimental import pallas as pl
from jax.experimental.pallas import tpu as pltpu
from jax.sharding import PartitionSpec as P

BF = jnp.bfloat16
F32 = jnp.float32

def nt(a, b):
    return lax.dot_general(a, b, (((1,), (1,)), ((), ())), preferred_element_type=F32)


def nn(a, b):
    return jnp.dot(a, b, preferred_element_type=F32)


def index_grids(h):
    return (lax.broadcasted_iota(jnp.int32, (h, h), 0), lax.broadcasted_iota(jnp.int32, (h, h), 1))


def quarter_identity(size):
    row, col = index_grids(size)
    return jnp.where(row == col, 0.25, 0.0).astype(F32)


def sign_of(branch_ref, step):
    return (2 * branch_ref[0, step] - 1).astype(F32)


def mixed_part(tile):
    h = tile.shape[0] // 2
    row, col = index_grids(h)
    return jnp.where(row <= col, tile[:h, :h], pltpu.roll(tile[h:, h:], 1, 0))


def symmetric_product(tile, mixed, below, c_last, grids):
    row, col = grids
    h = mixed.shape[0]
    c = jnp.where(row == h - 1, c_last, pltpu.roll(mixed, h - 1, 0))
    zero = jnp.zeros_like(mixed)
    stack = lambda a, b, d: jnp.concatenate(
        [jnp.concatenate([a, zero], axis=1), jnp.concatenate([b, d], axis=1)], axis=0
    ).astype(BF)
    straight = stack(jnp.where(row <= col, mixed, 0.0), below, jnp.where(row >= col, c, 0.0))
    flipped = stack(jnp.where(row < col, mixed, 0.0), below, jnp.where(row > col, c, 0.0))
    return (nn(tile, straight) + nt(tile, flipped)).astype(BF).astype(F32)


SIDE_ROWS = 8


def first_kernel(branch_hbm, x_hbm, sent0_ref, side_ref, held_ref, diag_ref, x_ref, rows_ref, branch_ref, sems, branch_sem):
    tiles, size = x_ref.shape[:2]
    h = size // 2
    loads = [pltpu.make_async_copy(x_hbm.at[s], x_ref.at[s], sems.at[s]) for s in range(tiles)]
    scalars = pltpu.make_async_copy(branch_hbm, branch_ref, branch_sem)
    for load in loads:
        load.start()
    scalars.start()
    loads[0].wait()
    x0 = x_ref[0]
    old = x0.astype(F32)
    sent0_ref[0, :h] = mixed_part(old).astype(BF)
    sent0_ref[0, h:] = x0[h : size - 1, :h]
    total = nt(x0, x0)
    for slot in range(1, tiles):
        loads[slot].wait()
        total += nt(x_ref[slot], x_ref[slot])
    scalars.wait()
    new = old + sign_of(branch_ref, 0) * (total - quarter_identity(size))
    diag_ref[...] = new
    held_ref[:h] = mixed_part(new).astype(BF)
    held_ref[h:] = new[h : size - 1, :h].astype(BF)
    rows_ref[...] = jnp.zeros(rows_ref.shape, F32)
    rows_ref[0:1] = old[size - 1 :, :h]
    rows_ref[1:2] = old[size - 1 :, h:]
    rows_ref[2:3] = new[size - 1 :, :h]
    rows_ref[3:4] = new[size - 1 :, h:]
    rows_ref[4:5] = new[size - 2 : size - 1, :h]
    side = rows_ref[...].astype(BF)
    for slot in range(side_ref.shape[0]):
        side_ref[slot] = side


def second_kernel(
    cluster, branch_ref, cols_ref, x_ref, diag_ref, held_ref, gathered_ref, side_ref, new_ref, sent_ref, rows_ref
):
    tiles, size = x_ref.shape[:2]
    h = size // 2
    sign, next_sign = sign_of(branch_ref, 0), sign_of(branch_ref, 1)
    grids = index_grids(h)
    diag = diag_ref[...]
    rounded = diag.astype(BF).astype(F32)
    squares = rounded * rounded
    x0 = x_ref[0]
    for slot in range(1, tiles):
        tile = x_ref[slot]
        partner = lax.rem(cols_ref[0, slot], cluster)
        side = side_ref[partner].astype(F32)
        rows = rows_ref.at[slot % rows_ref.shape[0]]
        rows[: size - 1] = gathered_ref[partner].astype(F32)
        rows[size - 1 :] = side[0:1]
        product = symmetric_product(tile, rows[:h], rows[h:], side[1:2], grids)
        new = tile.astype(F32) + sign * (nn(x0, tile) + product)
        new_ref[slot - 1] = new
        rounded = new.astype(BF).astype(F32)
        squares += rounded * rounded
    row, col = index_grids(size)
    trace = jnp.sum(jnp.where(row == col, diag - 0.25 * next_sign, 0.0) + next_sign * squares)
    lane = lax.broadcasted_iota(jnp.int32, (8, h), 1)
    left = jnp.full((8, h), trace, F32)
    line = jnp.zeros((8, h), F32)
    for k in range(3):
        piece = left.astype(BF).astype(F32)
        line = jnp.where(lane == k, piece, line)
        left = left - piece
    sent_ref[0] = held_ref[...]
    sent_ref[0, size - 2 :] = line[:1].astype(BF)


def third_kernel(
    cluster, branch_ref, cols_ref, diag_ref, new_ref, gathered_ref, side_ref,
    out_hbm, occupation_ref, out_ref, rows_ref, store_sems,
):
    tiles, size = out_ref.shape[:2]
    h = size // 2
    stores = [pltpu.make_async_copy(out_ref.at[s], out_hbm.at[s], store_sems.at[s]) for s in range(tiles)]
    sign = sign_of(branch_ref, 1)
    grids = index_grids(h)
    diag = diag_ref[...]
    r0 = diag.astype(BF)
    total = nt(r0, r0)
    for slot in range(1, tiles):
        new = new_ref[slot - 1]
        r = new.astype(BF)
        total += nt(r, r)
        partner = lax.rem(cols_ref[0, slot], cluster)
        side = side_ref[partner].astype(F32)
        rows = rows_ref.at[slot % rows_ref.shape[0]]
        rows[: size - 1] = gathered_ref[partner].astype(F32)
        rows[size - 2 : size - 1] = side[4:5]
        rows[size - 1 :] = side[2:3]
        product = symmetric_product(r, rows[:h], rows[h:], side[3:4], grids)
        out_ref[slot] = new + sign * (nn(r0, r) + product)
        stores[slot].start()
    out_ref[0] = diag + sign * (total - quarter_identity(size))
    stores[0].start()
    lines = jnp.zeros((1, h), F32)
    for member in range(cluster):
        lines += gathered_ref[member, size - 9 :].astype(F32)[7:]
    occupation_ref[0] = jnp.sum(lines) / (cluster * size) + 0.5
    for store in stores:
        store.wait()


S, V, H = (pl.BlockSpec(memory_space=m) for m in (pltpu.SMEM, pltpu.VMEM, pltpu.HBM))


def call(kernel, ins, outs, scratch, args, name):
    return pl.pallas_call(
        kernel,
        out_shape=[jax.ShapeDtypeStruct(shape, dtype) for shape, dtype, _ in outs],
        in_specs=list(ins),
        out_specs=[spec for _, _, spec in outs],
        scratch_shapes=scratch,
        compiler_params=pltpu.CompilerParams(vmem_limit_bytes=16 * 1024 * 1024),
        name=name,
    )(*args)


def shards(x_tiles, columns, branch):
    tiles, size = x_tiles.shape[1], x_tiles.shape[2]
    h = size // 2
    cluster = x_tiles.shape[0] * lax.axis_size("col")
    x = x_tiles.reshape(tiles, size, size)
    sems = pltpu.SemaphoreType.DMA((tiles,))
    most, rows = (size - 1, h), pltpu.VMEM((2, size, h), F32)

    sent0, side, held, diag = call(
        first_kernel,
        (H, H),
        [((1, *most), BF, V), ((cluster, SIDE_ROWS, h), BF, V), (most, BF, V), ((size, size), F32, V)],
        [
            pltpu.VMEM((tiles, size, size), BF),
            pltpu.VMEM((SIDE_ROWS, h), F32),
            pltpu.SMEM(branch.shape, jnp.int32),
            sems,
            pltpu.SemaphoreType.DMA,
        ],
        (pltpu.with_memory_space_constraint(branch, pltpu.HBM), pltpu.with_memory_space_constraint(x, pltpu.HBM)),
        "first",
    )
    sides = lax.all_to_all(side, "col", 0, 0, tiled=True)
    gathered0 = lax.all_gather(sent0, "col", axis=0, tiled=True)
    new, sent1 = call(
        lambda *refs: second_kernel(cluster, *refs),
        (S, S, V, V, V, V, V),
        [((tiles - 1, size, size), F32, V), ((1, *most), BF, V)],
        [rows],
        (branch, columns, x, diag, held, gathered0, sides),
        "second",
    )
    gathered1 = lax.all_gather(sent1, "col", axis=0, tiled=True)
    out, occupation = call(
        lambda *refs: third_kernel(cluster, *refs),
        (S, S, V, V, V, V),
        [((tiles, size, size), F32, H), ((1,), F32, S)],
        [pltpu.VMEM((tiles, size, size), F32), rows, sems],
        (branch, columns, diag, new, gathered1, sides),
        "third",
    )
    return out.reshape(x_tiles.shape), occupation


def solution(mesh):
    placed = (P(("row", "col"), None, None, None), P(("row", "col"), None), P("row", None))
    return jax.shard_map(
        shards,
        mesh=mesh,
        in_specs=placed,
        out_specs=(P(("row", "col"), None, None, None), P("row")),
        check_vma=False,
    )
```

time: 73.2 us -> 65.5 us (0.89)
  Pallas kernels: 13.8 us -> 7.98 us
  local copies, waits for them, and re-layouts: 1.9 us -> 0.01 us
    pallas_call x3, Pallas kernels: 13.8 us -> 7.98 us  [call(): pl.pallas_call(kernel, out_shape=[jax.ShapeDtypeStruct(shape, dtype) for...]
    unnamed x10 -> x6, local copies, waits for them, and re-layouts: 1.9 us -> 0.01 us
where the time goes in v2:
time: 65.5 us; the launch traced here: 65.3 us
  blocking collectives  38.4 us (59%)
  starting transfers between devices  18.2 us (28%)
  Pallas kernels  7.98 us (12%)
  between operations  0.68 us (1%)
    all_gather x1, blocking collectives, shards(): gathered0 = lax.all_gather(sent0, 'col', axis=0, tiled=True)  20.1 us
    all_gather x1, blocking collectives, shards(): gathered1 = lax.all_gather(sent1, 'col', axis=0, tiled=True)  18.3 us
    all_to_all x1, starting transfers between devices, shards(): sides = lax.all_to_all(side, 'col', 0, 0, tiled=True)  18.2 us
    pallas_call x3, Pallas kernels, call(): pl.pallas_call(kernel, out_shape=[jax.ShapeDtypeStruct(shape, dtype) for...  7.98 us
  transfers between devices with their start and end apart: 1, of which 0 were waited for; matrix products, arithmetic and copies ran while one was open for 0% of the time, Pallas kernels for 0%

profile of v2, /device:TPU:1, one launch (start us, length us, event | category | flops | bytes accessed | tf_op | source)
XLA Modules:
  0.0 65.3 jit_solution(15910643579603413594)
XLA Ops:
  0.6 0.0 copy-start.1
  0.6 0.0 copy-start
  0.6 0.0 copy-start.2
  0.7 3.1 %first.1 = (bf16[1,255,128]{2,1,0:T(8,128)(2,1)S(1)}, bf16[16,8,128]{2,1,0:T(8,128)(2,1)}, bf16[255,128]{1,0:T(8,128)(2,1)S(1)}, f32[256,256]{1,0:T(8,128)S(1)}) custom-call(s32[1,2]{1,0:T(1,128)} %refs_0_.3, bf16[8,256,256]{2,1,0:T(8,128)(2,1)} %bitcast.2), custom_call_target="tpu_custom_call" | custom-call | tf_op jit(solution)/shard_map/first/pallas_call | solution.py:162
  3.7 18.2 %all-to-all-start = ((bf16[16,8,128]{2,1,0:T(8,128)(2,1)}), bf16[16,8,128]{2,1,0:T(8,128)(2,1)S(1)}, u32[]{:S(2)}, u32[]{:S(2)}) async-start(bf16[16,8,128]{2,1,0:T(8,128)(2,1)} %get-tuple-element.13), calls=%async_computation | async-start | bytes 65536 | tf_op jit(solution)/shard_map/all_to_all | solution.py:195
  21.9 20.1 %all_gather.6.refs_5_ = bf16[16,255,128]{2,1,0:T(8,128)(2,1)S(1)} all-gather(bf16[1,255,128]{2,1,0:T(8,128)(2,1)S(1)} %get-tuple-element.12), channel_id=1, replica_groups=mesh['row'=64,'col'=16] {'col'}, dimensions={0}, use_global_device_ids=true | all-gather | bytes 1109760 | tf_op jit(solution)/shard_map/all_gather | solution.py:196
  42.0 0.0 all-to-all-done.refs_6_.refs_5_
  42.0 0.0 copy-done.1
  42.0 0.0 copy-done
  42.0 0.0 copy-done.2
  42.0 1.7 %second.1 = (f32[7,256,256]{2,1,0:T(8,128)S(1)}, bf16[1,255,128]{2,1,0:T(8,128)(2,1)S(1)}) custom-call(s32[1,2]{1,0:T(1,128)S(1)} %copy-done.1, s32[1,8]{1,0:T(1,128)S(1)} %copy-done.2, bf16[8,256,256]{2,1,0:T(8,128)(2,1)S(1)} %bitcast.3, f32[256,256]{1,0:T(8,128)S(1)} %get-tuple-element.10.refs_3_.refs_2_, bf16[255,128]{1,0:T(8,128)(2,1)S(1)} %get-tuple-element.11.refs_4_, ...), custom_call_target="tpu_custom_call" | custom-call | tf_op jit(solution)/shard_map/second/pallas_call | solution.py:162
  43.8 18.3 %all_gather.7.refs_4_ = bf16[16,255,128]{2,1,0:T(8,128)(2,1)S(1)} all-gather(bf16[1,255,128]{2,1,0:T(8,128)(2,1)S(1)} %get-tuple-element.15), channel_id=1, replica_groups=mesh['row'=64,'col'=16] {'col'}, dimensions={0}, use_global_device_ids=true | all-gather | bytes 1109760 | tf_op jit(solution)/shard_map/all_gather | solution.py:205
  62.1 3.2 %third.1 = (f32[8,256,256]{2,1,0:T(8,128)}, f32[1]{0:T(128)}) custom-call(s32[1,2]{1,0:T(1,128)S(1)} %copy-done.1, s32[1,8]{1,0:T(1,128)S(1)} %copy-done.2, f32[256,256]{1,0:T(8,128)S(1)} %get-tuple-element.10.refs_3_.refs_2_, f32[7,256,256]{2,1,0:T(8,128)S(1)} %get-tuple-element.14.refs_3_, bf16[16,255,128]{2,1,0:T(8,128)(2,1)S(1)} %all_gather.7.refs_4_, ...), custom_call_target="tpu_custom_call" | custom-call | tf_op jit(solution)/shard_map/third/pallas_call | solution.py:162
Async XLA Ops:
  0.6 41.4 %copy-start.1 = (s32[1,2]{1,0:T(1,128)S(1)}, s32[1,2]{1,0:T(1,128)}, u32[]{:S(2)}) copy-start(s32[1,2]{1,0:T(1,128)} %refs_0_.3) | copy-start | bytes 28
  0.6 41.4 %copy-start = (bf16[1,8,256,256]{3,2,1,0:T(8,128)(2,1)S(1)}, bf16[1,8,256,256]{3,2,1,0:T(8,128)(2,1)}, u32[]{:S(2)}) copy-start(bf16[1,8,256,256]{3,2,1,0:T(8,128)(2,1)} %param.3) | copy-start | bytes 3145732
  0.6 41.4 %copy-start.2 = (s32[1,8]{1,0:T(1,128)S(1)}, s32[1,8]{1,0:T(1,128)}, u32[]{:S(2)}) copy-start(s32[1,8]{1,0:T(1,128)} %refs_1_.3) | copy-start | bytes 100
  3.7 38.3 %all-to-all-start = ((bf16[16,8,128]{2,1,0:T(8,128)(2,1)}), bf16[16,8,128]{2,1,0:T(8,128)(2,1)S(1)}, u32[]{:S(2)}, u32[]{:S(2)}) async-start(bf16[16,8,128]{2,1,0:T(8,128)(2,1)} %get-tuple-element.13), calls=%async_computation | async-start | bytes 65536 | tf_op jit(solution)/shard_map/all_to_all | solution.py:195

commit v3 on v2

v3 whole, which is shorter than its diff:
```python
import jax
import jax.numpy as jnp
from jax import lax
from jax.experimental import pallas as pl
from jax.experimental.pallas import tpu as pltpu
from jax.sharding import PartitionSpec as P

BF = jnp.bfloat16
F32 = jnp.float32

def nt(a, b):
    return lax.dot_general(a, b, (((1,), (1,)), ((), ())), preferred_element_type=F32)


def nn(a, b):
    return jnp.dot(a, b, preferred_element_type=F32)


def index_grids(h):
    return (lax.broadcasted_iota(jnp.int32, (h, h), 0), lax.broadcasted_iota(jnp.int32, (h, h), 1))


def quarter_identity(size):
    row, col = index_grids(size)
    return jnp.where(row == col, 0.25, 0.0).astype(F32)


def sign_of(branch_ref, step):
    return (2 * branch_ref[0, step] - 1).astype(F32)


def mixed_part(tile):
    h = tile.shape[0] // 2
    row, col = index_grids(h)
    return jnp.where(row <= col, tile[:h, :h], pltpu.roll(tile[h:, h:], 1, 0))


def symmetric_product(tile, mixed, below, c_last, grids):
    row, col = grids
    h = mixed.shape[0]
    c = jnp.where(row == h - 1, c_last, pltpu.roll(mixed, h - 1, 0))
    above = jnp.concatenate([jnp.where(row <= col, mixed, mixed.T), below.T], axis=1)
    under = jnp.concatenate([below, jnp.where(row >= col, c, c.T)], axis=1)
    return nn(tile, jnp.concatenate([above, under], axis=0).astype(BF)).astype(BF).astype(F32)


SIDE_ROWS = 8


def first_kernel(branch_hbm, x_hbm, sent_ref, diag_ref, x_ref, branch_ref, sems, branch_sem):
    tiles, size = x_ref.shape[:2]
    h = size // 2
    loads = [pltpu.make_async_copy(x_hbm.at[s], x_ref.at[s], sems.at[s]) for s in range(tiles)]
    scalars = pltpu.make_async_copy(branch_hbm, branch_ref, branch_sem)
    for load in loads:
        load.start()
    scalars.start()
    loads[0].wait()
    x0 = x_ref[0]
    old = x0.astype(F32)
    sent_ref[0, :h] = mixed_part(old).astype(BF)
    sent_ref[0, h:size] = x0[h:, :h]
    total = nt(x0, x0)
    for slot in range(1, tiles):
        loads[slot].wait()
        total += nt(x_ref[slot], x_ref[slot])
    scalars.wait()
    new = old + sign_of(branch_ref, 0) * (total - quarter_identity(size))
    diag_ref[...] = new
    sent_ref[0, size : size + h] = mixed_part(new).astype(BF)
    sent_ref[0, size + h : 2 * size - 2] = new[h : size - 2, :h].astype(BF)
    sent_ref[0, 2 * size - 2 :] = old[size - 1 :, h:].astype(BF)


def second_kernel(cluster, branch_ref, cols_ref, x_ref, diag_ref, gathered_ref, new_ref, side_ref, rows_ref):
    tiles, size = x_ref.shape[:2]
    h = size // 2
    sign, next_sign = sign_of(branch_ref, 0), sign_of(branch_ref, 1)
    grids = index_grids(h)
    diag = diag_ref[...]
    rounded = diag.astype(BF).astype(F32)
    squares = rounded * rounded
    x0 = x_ref[0]
    for slot in range(1, tiles):
        tile = x_ref[slot]
        partner = lax.rem(cols_ref[0, slot], cluster // 2)
        rows = gathered_ref[partner, :size].astype(F32)
        c_last = gathered_ref[partner, 2 * size - 8 :].astype(F32)[6:]
        product = symmetric_product(tile, rows[:h], rows[h:], c_last, grids)
        new = tile.astype(F32) + sign * (nn(x0, tile) + product)
        new_ref[slot - 1] = new
        rounded = new.astype(BF).astype(F32)
        squares += rounded * rounded
    row, col = index_grids(size)
    trace = jnp.sum(jnp.where(row == col, diag - 0.25 * next_sign, 0.0) + next_sign * squares)
    lane = lax.broadcasted_iota(jnp.int32, (SIDE_ROWS, h), 1)
    left = jnp.full((SIDE_ROWS, h), trace, F32)
    line = jnp.zeros((SIDE_ROWS, h), F32)
    for k in range(3):
        piece = left.astype(BF).astype(F32)
        line = jnp.where(lane == k, piece, line)
        left = left - piece
    rows_ref[...] = line
    rows_ref[0:1] = diag[size - 2 : size - 1, :h]
    rows_ref[1:2] = diag[size - 1 :, :h]
    rows_ref[2:3] = diag[size - 1 :, h:]
    side = rows_ref[...].astype(BF)
    for slot in range(side_ref.shape[0]):
        side_ref[slot] = side


def third_kernel(
    cluster, branch_ref, cols_ref, diag_ref, new_ref, gathered_ref, side_ref,
    out_hbm, occupation_ref, out_ref, rows_ref, store_sems,
):
    tiles, size = out_ref.shape[:2]
    h = size // 2
    stores = [pltpu.make_async_copy(out_ref.at[s], out_hbm.at[s], store_sems.at[s]) for s in range(tiles)]
    sign = sign_of(branch_ref, 1)
    grids = index_grids(h)
    diag = diag_ref[...]
    r0 = diag.astype(BF)
    total = nt(r0, r0)
    for slot in range(1, tiles):
        new = new_ref[slot - 1]
        r = new.astype(BF)
        total += nt(r, r)
        column = cols_ref[0, slot]
        side = side_ref[lax.rem(column, cluster)].astype(F32)
        rows = rows_ref.at[slot % rows_ref.shape[0]]
        rows[: size - 1] = gathered_ref[lax.rem(column, cluster // 2), size:].astype(F32)
        rows[size - 2 :] = side[0:2]
        product = symmetric_product(r, rows[:h], rows[h:], side[2:3], grids)
        out_ref[slot] = new + sign * (nn(r0, r) + product)
        stores[slot].start()
    out_ref[0] = diag + sign * (total - quarter_identity(size))
    stores[0].start()
    lines = jnp.zeros((SIDE_ROWS, h), F32)
    for member in range(cluster):
        lines += side_ref[member].astype(F32)
    occupation_ref[0] = jnp.sum(lines[3:4]) / (cluster * size) + 0.5
    for store in stores:
        store.wait()


S, V, H = (pl.BlockSpec(memory_space=m) for m in (pltpu.SMEM, pltpu.VMEM, pltpu.HBM))


def call(kernel, ins, outs, scratch, args, name):
    return pl.pallas_call(
        kernel,
        out_shape=[jax.ShapeDtypeStruct(shape, dtype) for shape, dtype, _ in outs],
        in_specs=list(ins),
        out_specs=[spec for _, _, spec in outs],
        scratch_shapes=scratch,
        compiler_params=pltpu.CompilerParams(vmem_limit_bytes=16 * 1024 * 1024),
        name=name,
    )(*args)


def shards(x_tiles, columns, branch):
    tiles, size = x_tiles.shape[1], x_tiles.shape[2]
    h = size // 2
    cluster = x_tiles.shape[0] * lax.axis_size("col")
    x = x_tiles.reshape(tiles, size, size)
    sems = pltpu.SemaphoreType.DMA((tiles,))
    tile32, fewer = (size, size), (tiles - 1, size, size)
    halves = [list(range(cluster // 2)), list(range(cluster // 2, cluster))]
    across = [(i, (i + cluster // 2) % cluster) for i in range(cluster)]

    sent, diag = call(
        first_kernel,
        (H, H),
        [((1, 2 * size - 1, h), BF, V), (tile32, F32, V)],
        [pltpu.VMEM((tiles, size, size), BF), pltpu.SMEM(branch.shape, jnp.int32), sems, pltpu.SemaphoreType.DMA],
        (pltpu.with_memory_space_constraint(branch, pltpu.HBM), pltpu.with_memory_space_constraint(x, pltpu.HBM)),
        "first",
    )
    crossed = lax.ppermute(sent, "col", across)
    gathered = lax.all_gather(crossed, "col", axis=0, tiled=True, axis_index_groups=halves)
    new, side = call(
        lambda *refs: second_kernel(cluster, *refs),
        (S, S, V, V, V),
        [(fewer, F32, V), ((cluster, SIDE_ROWS, h), BF, V)],
        [pltpu.VMEM((SIDE_ROWS, h), F32)],
        (branch, columns, x, diag, gathered),
        "second",
    )
    sides = lax.all_to_all(side, "col", 0, 0, tiled=True)
    out, occupation = call(
        lambda *refs: third_kernel(cluster, *refs),
        (S, S, V, V, V, V),
        [((tiles, size, size), F32, H), ((1,), F32, S)],
        [pltpu.VMEM((tiles, size, size), F32), pltpu.VMEM((2, size, h), F32), sems],
        (branch, columns, diag, new, gathered, sides),
        "third",
    )
    return out.reshape(x_tiles.shape), occupation


def solution(mesh):
    placed = (P(("row", "col"), None, None, None), P(("row", "col"), None), P("row", None))
    return jax.shard_map(
        shards,
        mesh=mesh,
        in_specs=placed,
        out_specs=(P(("row", "col"), None, None, None), P("row")),
        check_vma=False,
    )
```

time: 65.5 us -> 62.3 us (0.951)
  starting transfers between devices: 18.2 us -> 15.1 us
  waiting for transfers between devices: 0.01 us -> 2.34 us
  blocking collectives: 38.4 us -> 36.6 us
  Pallas kernels: 7.98 us -> 7.28 us
    all_to_all x1 -> x0, starting transfers between devices: 18.2 us -> none  [shards(): sides = lax.all_to_all(side, 'col', 0, 0, tiled=True)]
    ppermute x0 -> x1, starting transfers between devices: none -> 15.1 us  [shards(): crossed = lax.ppermute(sent, 'col', across)]
    all_gather x2 -> x1, blocking collectives: 38.4 us -> 26.6 us  [shards(): lax.all_gather(crossed, 'col', axis=0, tiled=True, axis_index_groups=halves)]
    all_to_all x0 -> x1, blocking collectives: none -> 10 us  [shards(): sides = lax.all_to_all(side, 'col', 0, 0, tiled=True)]
    ppermute x0 -> x1, waiting for transfers between devices: none -> 2.34 us  [shards(): crossed = lax.ppermute(sent, 'col', across)]
    pallas_call x3, Pallas kernels: 7.98 us -> 7.28 us  [call(): pl.pallas_call(kernel, out_shape=[jax.ShapeDtypeStruct(shape, dtype) for...]
  transfers between devices with their start and end apart: 1 -> 1, of which waited for: 0 -> 1; matrix products, arithmetic and copies ran while one was open for 0% -> 0% of each run, Pallas kernels for 0% -> 0%
where the time goes in v3:
time: 62.3 us; the launch traced here: 62.1 us
  blocking collectives  36.6 us (59%)
  starting transfers between devices  15.1 us (24%)
  Pallas kernels  7.28 us (12%)
  waiting for transfers between devices  2.34 us (4%)
  between operations  0.68 us (1%)
    all_gather x1, blocking collectives, shards(): lax.all_gather(crossed, 'col', axis=0, tiled=True, axis_index_groups=halves)  26.6 us
    ppermute x1, starting transfers between devices, shards(): crossed = lax.ppermute(sent, 'col', across)  15.1 us
    all_to_all x1, blocking collectives, shards(): sides = lax.all_to_all(side, 'col', 0, 0, tiled=True)  10 us
    pallas_call x3, Pallas kernels, call(): pl.pallas_call(kernel, out_shape=[jax.ShapeDtypeStruct(shape, dtype) for...  7.28 us
    ppermute x1, waiting for transfers between devices, shards(): crossed = lax.ppermute(sent, 'col', across)  2.34 us
  transfers between devices with their start and end apart: 1, of which 1 were waited for; matrix products, arithmetic and copies ran while one was open for 0% of the time, Pallas kernels for 0%

profile of v3, /device:TPU:1, one launch (start us, length us, event | category | flops | bytes accessed | tf_op | source)
XLA Modules:
  0.0 62.1 jit_solution(15528461132471491917)
XLA Ops:
  0.6 0.0 copy-start.1
  0.6 0.0 copy-start
  0.6 0.0 copy-start.2
  0.7 2.4 %first.1 = (bf16[1,511,128]{2,1,0:T(8,128)(2,1)S(1)}, f32[256,256]{1,0:T(8,128)S(1)}) custom-call(s32[1,2]{1,0:T(1,128)} %refs_0_.3, bf16[8,256,256]{2,1,0:T(8,128)(2,1)} %bitcast.2), custom_call_target="tpu_custom_call" | custom-call | tf_op jit(solution)/shard_map/first/pallas_call | solution.py:150
  3.1 15.1 %collective-permute-start = (bf16[1,511,128]{2,1,0:T(8,128)(2,1)S(1)}, bf16[1,511,128]{2,1,0:T(8,128)(2,1)S(1)}, u32[]{:S(2)}, u32[]{:S(2)}) collective-permute-start(bf16[1,511,128]{2,1,0:T(8,128)(2,1)S(1)} %get-tuple-element.9), channel_id=1, source_target_pairs={{0,8},{1,9},{2,10},{3,11},{4,12},{5,13},{6,14},{7,15},{8,0},{9,1},... | collective-permute-start | bytes 392456 | tf_op jit(solution)/shard_map/ppermute | solution.py:179
  18.2 2.3 %collective-permute-done = bf16[1,511,128]{2,1,0:T(8,128)(2,1)S(1)} collective-permute-done((bf16[1,511,128]{2,1,0:T(8,128)(2,1)S(1)}, bf16[1,511,128]{2,1,0:T(8,128)(2,1)S(1)}, u32[]{:S(2)}, u32[]{:S(2)}) %collective-permute-start) | collective-permute-done | bytes 130848 | tf_op jit(solution)/shard_map/ppermute | solution.py:179
  20.6 26.6 %all_gather.3.refs_4_ = bf16[8,511,128]{2,1,0:T(8,128)(2,1)S(1)} all-gather(bf16[1,511,128]{2,1,0:T(8,128)(2,1)S(1)} %collective-permute-done), channel_id=1, replica_groups={{0,1,2,3,4,5,6,7},{8,9,10,11,12,13,14,15},{16,17,18,19,20,21,22,23},{24..., dimensions={0}, use_global_device_ids=true | all-gather | bytes 1177344 | tf_op jit(solution)/shard_map/all_gather | solution.py:180
  47.2 0.0 copy-done.1
  47.2 0.0 copy-done
  47.2 0.0 copy-done.2
  47.2 1.8 %second.1 = (f32[7,256,256]{2,1,0:T(8,128)S(1)}, bf16[16,8,128]{2,1,0:T(8,128)(2,1)S(1)}) custom-call(s32[1,2]{1,0:T(1,128)S(1)} %copy-done.1, s32[1,8]{1,0:T(1,128)S(1)} %copy-done.2, bf16[8,256,256]{2,1,0:T(8,128)(2,1)S(1)} %bitcast.3, f32[256,256]{1,0:T(8,128)S(1)} %get-tuple-element.8.refs_3_.refs_2_, bf16[8,511,128]{2,1,0:T(8,128)(2,1)S(1)} %all_gather.3.refs_4_), custom_call_target="tpu_custom_call" | custom-call | tf_op jit(solution)/shard_map/second/pallas_call | solution.py:150
  49.0 10.0 %all_to_all.5.refs_5_ = bf16[16,8,128]{2,1,0:T(8,128)(2,1)S(1)} all-to-all(bf16[16,8,128]{2,1,0:T(8,128)(2,1)S(1)} %get-tuple-element.11), channel_id=1, replica_groups=mesh['row'=64,'col'=16] {'col'}, dimensions={0} | all-to-all | bytes 65536 | tf_op jit(solution)/shard_map/all_to_all | solution.py:189
  59.0 3.1 %third.1 = (f32[8,256,256]{2,1,0:T(8,128)}, f32[1]{0:T(128)}) custom-call(s32[1,2]{1,0:T(1,128)S(1)} %copy-done.1, s32[1,8]{1,0:T(1,128)S(1)} %copy-done.2, f32[256,256]{1,0:T(8,128)S(1)} %get-tuple-element.8.refs_3_.refs_2_, f32[7,256,256]{2,1,0:T(8,128)S(1)} %get-tuple-element.10.refs_3_, bf16[8,511,128]{2,1,0:T(8,128)(2,1)S(1)} %all_gather.3.refs_4_, ...), custom_call_target="tpu_custom_call" | custom-call | tf_op jit(solution)/shard_map/third/pallas_call | solution.py:150
Async XLA Ops:
  0.6 46.5 %copy-start.1 = (s32[1,2]{1,0:T(1,128)S(1)}, s32[1,2]{1,0:T(1,128)}, u32[]{:S(2)}) copy-start(s32[1,2]{1,0:T(1,128)} %refs_0_.3) | copy-start | bytes 28
  0.6 46.5 %copy-start = (bf16[1,8,256,256]{3,2,1,0:T(8,128)(2,1)S(1)}, bf16[1,8,256,256]{3,2,1,0:T(8,128)(2,1)}, u32[]{:S(2)}) copy-start(bf16[1,8,256,256]{3,2,1,0:T(8,128)(2,1)} %param.3) | copy-start | bytes 3145732
  0.6 46.5 %copy-start.2 = (s32[1,8]{1,0:T(1,128)S(1)}, s32[1,8]{1,0:T(1,128)}, u32[]{:S(2)}) copy-start(s32[1,8]{1,0:T(1,128)} %refs_1_.3) | copy-start | bytes 100
  3.1 17.5 %collective-permute-start = (bf16[1,511,128]{2,1,0:T(8,128)(2,1)S(1)}, bf16[1,511,128]{2,1,0:T(8,128)(2,1)S(1)}, u32[]{:S(2)}, u32[]{:S(2)}) collective-permute-start(bf16[1,511,128]{2,1,0:T(8,128)(2,1)S(1)} %get-tuple-element.9), channel_id=1, source_target_pairs={{0,8},{1,9},{2,10},{3,11},{4,12},{5,13},{6,14},{7,15},{8,0},{9,1},... | collective-permute-start | bytes 392456 | tf_op jit(solution)/shard_map/ppermute | solution.py:179

commit v4 on v3

--- a/solution.py
+++ b/solution.py
@@ -44,7 +44,11 @@
     return nn(tile, jnp.concatenate([above, under], axis=0).astype(BF)).astype(BF).astype(F32)
 
 
-SIDE_ROWS = 8
+SIDE_ROWS, ASIDE = 16, 8
+
+
+def holder_of(column, cluster):
+    return lax.bitwise_xor(lax.rem(column, cluster // 2), cluster // 4)
 
 
 def first_kernel(branch_hbm, x_hbm, sent_ref, diag_ref, x_ref, branch_ref, sems, branch_sem):
@@ -60,16 +64,19 @@
     old = x0.astype(F32)
     sent_ref[0, :h] = mixed_part(old).astype(BF)
     sent_ref[0, h:size] = x0[h:, :h]
-    total = nt(x0, x0)
-    for slot in range(1, tiles):
-        loads[slot].wait()
-        total += nt(x_ref[slot], x_ref[slot])
+    total = None
+    for part in (range(tiles // 2), range(tiles // 2, tiles)):
+        for slot in part:
+            if slot:
+                loads[slot].wait()
+        wide = jnp.concatenate([x_ref[slot] for slot in part], axis=1)
+        total = nt(wide, wide) if total is None else total + nt(wide, wide)
     scalars.wait()
     new = old + sign_of(branch_ref, 0) * (total - quarter_identity(size))
     diag_ref[...] = new
     sent_ref[0, size : size + h] = mixed_part(new).astype(BF)
-    sent_ref[0, size + h : 2 * size - 2] = new[h : size - 2, :h].astype(BF)
-    sent_ref[0, 2 * size - 2 :] = old[size - 1 :, h:].astype(BF)
+    sent_ref[0, size + h : 2 * size - ASIDE] = new[h : size - ASIDE, :h].astype(BF)
+    sent_ref[0, 2 * size - ASIDE :] = old[size - 1 :, h:].astype(BF)
 
 
 def second_kernel(cluster, branch_ref, cols_ref, x_ref, diag_ref, gathered_ref, new_ref, side_ref, rows_ref):
@@ -83,9 +90,9 @@
     x0 = x_ref[0]
     for slot in range(1, tiles):
         tile = x_ref[slot]
-        partner = lax.rem(cols_ref[0, slot], cluster // 2)
+        partner = holder_of(cols_ref[0, slot], cluster)
         rows = gathered_ref[partner, :size].astype(F32)
-        c_last = gathered_ref[partner, 2 * size - 8 :].astype(F32)[6:]
+        c_last = gathered_ref[partner, 2 * size - ASIDE :].astype(F32)
         product = symmetric_product(tile, rows[:h], rows[h:], c_last, grids)
         new = tile.astype(F32) + sign * (nn(x0, tile) + product)
         new_ref[slot - 1] = new
@@ -101,9 +108,8 @@
         line = jnp.where(lane == k, piece, line)
         left = left - piece
     rows_ref[...] = line
-    rows_ref[0:1] = diag[size - 2 : size - 1, :h]
-    rows_ref[1:2] = diag[size - 1 :, :h]
-    rows_ref[2:3] = diag[size - 1 :, h:]
+    rows_ref[:ASIDE] = diag[size - ASIDE :, :h]
+    rows_ref[ASIDE : ASIDE + 1] = diag[size - 1 :, h:]
     side = rows_ref[...].astype(BF)
     for slot in range(side_ref.shape[0]):
         side_ref[slot] = side
@@ -111,11 +117,17 @@
 
 def third_kernel(
     cluster, branch_ref, cols_ref, diag_ref, new_ref, gathered_ref, side_ref,
-    out_hbm, occupation_ref, out_ref, rows_ref, store_sems,
+    out_hbm, occupation_hbm, out_ref, occupation_ref, store_sems, occupation_sem,
 ):
     tiles, size = out_ref.shape[:2]
     h = size // 2
     stores = [pltpu.make_async_copy(out_ref.at[s], out_hbm.at[s], store_sems.at[s]) for s in range(tiles)]
+    lines = jnp.zeros((SIDE_ROWS, h), F32)
+    for member in range(cluster):
+        lines += side_ref[member].astype(F32)
+    occupation_ref[0] = jnp.sum(lines[ASIDE + 1 : ASIDE + 2]) / (cluster * size) + 0.5
+    stores.append(pltpu.make_async_copy(occupation_ref, occupation_hbm, occupation_sem))
+    stores[tiles].start()
     sign = sign_of(branch_ref, 1)
     grids = index_grids(h)
     diag = diag_ref[...]
@@ -127,18 +139,13 @@
         total += nt(r, r)
         column = cols_ref[0, slot]
         side = side_ref[lax.rem(column, cluster)].astype(F32)
-        rows = rows_ref.at[slot % rows_ref.shape[0]]
-        rows[: size - 1] = gathered_ref[lax.rem(column, cluster // 2), size:].astype(F32)
-        rows[size - 2 :] = side[0:2]
-        product = symmetric_product(r, rows[:h], rows[h:], side[2:3], grids)
+        rows = gathered_ref[holder_of(column, cluster), size : 2 * size - ASIDE].astype(F32)
+        below = jnp.concatenate([rows[h:], side[:ASIDE]], axis=0)
+        product = symmetric_product(r, rows[:h], below, side[ASIDE : ASIDE + 1], grids)
         out_ref[slot] = new + sign * (nn(r0, r) + product)
         stores[slot].start()
     out_ref[0] = diag + sign * (total - quarter_identity(size))
     stores[0].start()
-    lines = jnp.zeros((SIDE_ROWS, h), F32)
-    for member in range(cluster):
-        lines += side_ref[member].astype(F32)
-    occupation_ref[0] = jnp.sum(lines[3:4]) / (cluster * size) + 0.5
     for store in stores:
         store.wait()
 
@@ -166,12 +173,12 @@
     sems = pltpu.SemaphoreType.DMA((tiles,))
     tile32, fewer = (size, size), (tiles - 1, size, size)
     halves = [list(range(cluster // 2)), list(range(cluster // 2, cluster))]
-    across = [(i, (i + cluster // 2) % cluster) for i in range(cluster)]
+    across = [(i, i ^ (cluster // 2 + cluster // 4)) for i in range(cluster)]
 
     sent, diag = call(
         first_kernel,
         (H, H),
-        [((1, 2 * size - 1, h), BF, V), (tile32, F32, V)],
+        [((1, 2 * size - ASIDE + 1, h), BF, V), (tile32, F32, V)],
         [pltpu.VMEM((tiles, size, size), BF), pltpu.SMEM(branch.shape, jnp.int32), sems, pltpu.SemaphoreType.DMA],
         (pltpu.with_memory_space_constraint(branch, pltpu.HBM), pltpu.with_memory_space_constraint(x, pltpu.HBM)),
         "first",
@@ -190,8 +197,8 @@
     out, occupation = call(
         lambda *refs: third_kernel(cluster, *refs),
         (S, S, V, V, V, V),
-        [((tiles, size, size), F32, H), ((1,), F32, S)],
-        [pltpu.VMEM((tiles, size, size), F32), pltpu.VMEM((2, size, h), F32), sems],
+        [((tiles, size, size), F32, H), ((1,), F32, H)],
+        [pltpu.VMEM((tiles, size, size), F32), pltpu.SMEM((1,), F32), sems, pltpu.SemaphoreType.DMA],
         (branch, columns, diag, new, gathered, sides),
         "third",
     )

time: 62.3 us -> 60.7 us (0.974)
  blocking collectives: 36.6 us -> 34.2 us
  starting transfers between devices: 15.1 us -> 16.9 us
  Pallas kernels: 7.28 us -> 6.31 us
    all_gather x1, blocking collectives: 26.6 us -> 20.1 us  [shards(): lax.all_gather(crossed, 'col', axis=0, tiled=True, axis_index_groups=halves)]
    all_to_all x1, blocking collectives: 10 us -> 14.1 us  [shards(): sides = lax.all_to_all(side, 'col', 0, 0, tiled=True)]
    ppermute x1, starting transfers between devices: 15.1 us -> 16.9 us  [shards(): crossed = lax.ppermute(sent, 'col', across)]
    pallas_call x3, Pallas kernels: 7.28 us -> 6.31 us  [call(): pl.pallas_call(kernel, out_shape=[jax.ShapeDtypeStruct(shape, dtype) for...]
where the time goes in v4:
time: 60.7 us; the launch traced here: 60.5 us
  blocking collectives  34.2 us (56%)
  starting transfers between devices  16.9 us (28%)
  Pallas kernels  6.31 us (10%)
  waiting for transfers between devices  2.39 us (4%)
  between operations  0.68 us (1%)
    all_gather x1, blocking collectives, shards(): lax.all_gather(crossed, 'col', axis=0, tiled=True, axis_index_groups=halves)  20.1 us
    ppermute x1, starting transfers between devices, shards(): crossed = lax.ppermute(sent, 'col', across)  16.9 us
    all_to_all x1, blocking collectives, shards(): sides = lax.all_to_all(side, 'col', 0, 0, tiled=True)  14.1 us
    pallas_call x3, Pallas kernels, call(): pl.pallas_call(kernel, out_shape=[jax.ShapeDtypeStruct(shape, dtype) for...  6.31 us
    ppermute x1, waiting for transfers between devices, shards(): crossed = lax.ppermute(sent, 'col', across)  2.39 us
  transfers between devices with their start and end apart: 1, of which 1 were waited for; matrix products, arithmetic and copies ran while one was open for 0% of the time, Pallas kernels for 0%

profile of v4, /device:TPU:1, one launch (start us, length us, event | category | flops | bytes accessed | tf_op | source)
XLA Modules:
  0.0 60.5 jit_solution(11832136058201301698)
XLA Ops:
  0.6 0.0 copy-start.1
  0.6 0.0 copy-start
  0.6 0.0 copy-start.2
  0.7 2.0 %first.1 = (bf16[1,505,128]{2,1,0:T(8,128)(2,1)S(1)}, f32[256,256]{1,0:T(8,128)S(1)}) custom-call(s32[1,2]{1,0:T(1,128)} %refs_0_.3, bf16[8,256,256]{2,1,0:T(8,128)(2,1)} %bitcast.2), custom_call_target="tpu_custom_call" | custom-call | tf_op jit(solution)/shard_map/first/pallas_call | solution.py:157
  2.6 16.9 %collective-permute-start = (bf16[1,505,128]{2,1,0:T(8,128)(2,1)S(1)}, bf16[1,505,128]{2,1,0:T(8,128)(2,1)S(1)}, u32[]{:S(2)}, u32[]{:S(2)}) collective-permute-start(bf16[1,505,128]{2,1,0:T(8,128)(2,1)S(1)} %get-tuple-element.9), channel_id=1, source_target_pairs={{0,12},{1,13},{2,14},{3,15},{4,8},{5,9},{6,10},{7,11},{8,4},{9,5},... | collective-permute-start | bytes 387848 | tf_op jit(solution)/shard_map/ppermute | solution.py:186
  19.6 2.4 %collective-permute-done = bf16[1,505,128]{2,1,0:T(8,128)(2,1)S(1)} collective-permute-done((bf16[1,505,128]{2,1,0:T(8,128)(2,1)S(1)}, bf16[1,505,128]{2,1,0:T(8,128)(2,1)S(1)}, u32[]{:S(2)}, u32[]{:S(2)}) %collective-permute-start) | collective-permute-done | bytes 129312 | tf_op jit(solution)/shard_map/ppermute | solution.py:186
  22.0 20.1 %all_gather.3.refs_4_ = bf16[8,505,128]{2,1,0:T(8,128)(2,1)S(1)} all-gather(bf16[1,505,128]{2,1,0:T(8,128)(2,1)S(1)} %collective-permute-done), channel_id=1, replica_groups={{0,1,2,3,4,5,6,7},{8,9,10,11,12,13,14,15},{16,17,18,19,20,21,22,23},{24..., dimensions={0}, use_global_device_ids=true | all-gather | bytes 1163520 | tf_op jit(solution)/shard_map/all_gather | solution.py:187
  42.1 0.0 copy-done.1
  42.1 0.0 copy-done
  42.1 0.0 copy-done.2
  42.1 1.8 %second.1 = (f32[7,256,256]{2,1,0:T(8,128)S(1)}, bf16[16,16,128]{2,1,0:T(8,128)(2,1)S(1)}) custom-call(s32[1,2]{1,0:T(1,128)S(1)} %copy-done.1, s32[1,8]{1,0:T(1,128)S(1)} %copy-done.2, bf16[8,256,256]{2,1,0:T(8,128)(2,1)S(1)} %bitcast.3, f32[256,256]{1,0:T(8,128)S(1)} %get-tuple-element.8.refs_3_.refs_2_, bf16[8,505,128]{2,1,0:T(8,128)(2,1)S(1)} %all_gather.3.refs_4_), custom_call_target="tpu_custom_call" | custom-call | tf_op jit(solution)/shard_map/second/pallas_call | solution.py:157
  43.9 14.1 %all_to_all.5.refs_5_ = bf16[16,16,128]{2,1,0:T(8,128)(2,1)S(1)} all-to-all(bf16[16,16,128]{2,1,0:T(8,128)(2,1)S(1)} %get-tuple-element.11), channel_id=1, replica_groups=mesh['row'=64,'col'=16] {'col'}, dimensions={0} | all-to-all | bytes 131072 | tf_op jit(solution)/shard_map/all_to_all | solution.py:196
  57.9 2.6 %third.1 = (f32[8,256,256]{2,1,0:T(8,128)}, f32[1]{0:T(128)}) custom-call(s32[1,2]{1,0:T(1,128)S(1)} %copy-done.1, s32[1,8]{1,0:T(1,128)S(1)} %copy-done.2, f32[256,256]{1,0:T(8,128)S(1)} %get-tuple-element.8.refs_3_.refs_2_, f32[7,256,256]{2,1,0:T(8,128)S(1)} %get-tuple-element.10.refs_3_, bf16[8,505,128]{2,1,0:T(8,128)(2,1)S(1)} %all_gather.3.refs_4_, ...), custom_call_target="tpu_custom_call" | custom-call | tf_op jit(solution)/shard_map/third/pallas_call | solution.py:157
Async XLA Ops:
  0.6 41.4 %copy-start.1 = (s32[1,2]{1,0:T(1,128)S(1)}, s32[1,2]{1,0:T(1,128)}, u32[]{:S(2)}) copy-start(s32[1,2]{1,0:T(1,128)} %refs_0_.3) | copy-start | bytes 28
  0.6 41.4 %copy-start = (bf16[1,8,256,256]{3,2,1,0:T(8,128)(2,1)S(1)}, bf16[1,8,256,256]{3,2,1,0:T(8,128)(2,1)}, u32[]{:S(2)}) copy-start(bf16[1,8,256,256]{3,2,1,0:T(8,128)(2,1)} %param.3) | copy-start | bytes 3145732
  0.6 41.4 %copy-start.2 = (s32[1,8]{1,0:T(1,128)S(1)}, s32[1,8]{1,0:T(1,128)}, u32[]{:S(2)}) copy-start(s32[1,8]{1,0:T(1,128)} %refs_1_.3) | copy-start | bytes 100
  2.6 19.3 %collective-permute-start = (bf16[1,505,128]{2,1,0:T(8,128)(2,1)S(1)}, bf16[1,505,128]{2,1,0:T(8,128)(2,1)S(1)}, u32[]{:S(2)}, u32[]{:S(2)}) collective-permute-start(bf16[1,505,128]{2,1,0:T(8,128)(2,1)S(1)} %get-tuple-element.9), channel_id=1, source_target_pairs={{0,12},{1,13},{2,14},{3,15},{4,8},{5,9},{6,10},{7,11},{8,4},{9,5},... | collective-permute-start | bytes 387848 | tf_op jit(solution)/shard_map/ppermute | solution.py:186

commit v5 on v4

--- a/solution.py
+++ b/solution.py
@@ -35,16 +35,16 @@
     return jnp.where(row <= col, tile[:h, :h], pltpu.roll(tile[h:, h:], 1, 0))
 
 
-def symmetric_product(tile, mixed, below, c_last, grids):
+def unfolded(mixed, below, c_last, grids):
     row, col = grids
     h = mixed.shape[0]
     c = jnp.where(row == h - 1, c_last, pltpu.roll(mixed, h - 1, 0))
     above = jnp.concatenate([jnp.where(row <= col, mixed, mixed.T), below.T], axis=1)
     under = jnp.concatenate([below, jnp.where(row >= col, c, c.T)], axis=1)
-    return nn(tile, jnp.concatenate([above, under], axis=0).astype(BF)).astype(BF).astype(F32)
-
-
-SIDE_ROWS, ASIDE = 16, 8
+    return jnp.concatenate([above, under], axis=0).astype(BF)
+
+
+SIDE_ROWS, ASIDE, NORMS = 24, 8, 16
 
 
 def holder_of(column, cluster):
@@ -79,38 +79,60 @@
     sent_ref[0, 2 * size - ASIDE :] = old[size - 1 :, h:].astype(BF)
 
 
-def second_kernel(cluster, branch_ref, cols_ref, x_ref, diag_ref, gathered_ref, new_ref, side_ref, rows_ref):
-    tiles, size = x_ref.shape[:2]
-    h = size // 2
-    sign, next_sign = sign_of(branch_ref, 0), sign_of(branch_ref, 1)
-    grids = index_grids(h)
-    diag = diag_ref[...]
+def diagonal_trace(diag, sign):
+    row, col = index_grids(diag.shape[0])
     rounded = diag.astype(BF).astype(F32)
-    squares = rounded * rounded
-    x0 = x_ref[0]
-    for slot in range(1, tiles):
-        tile = x_ref[slot]
-        partner = holder_of(cols_ref[0, slot], cluster)
-        rows = gathered_ref[partner, :size].astype(F32)
-        c_last = gathered_ref[partner, 2 * size - ASIDE :].astype(F32)
-        product = symmetric_product(tile, rows[:h], rows[h:], c_last, grids)
-        new = tile.astype(F32) + sign * (nn(x0, tile) + product)
-        new_ref[slot - 1] = new
-        rounded = new.astype(BF).astype(F32)
-        squares += rounded * rounded
-    row, col = index_grids(size)
-    trace = jnp.sum(jnp.where(row == col, diag - 0.25 * next_sign, 0.0) + next_sign * squares)
-    lane = lax.broadcasted_iota(jnp.int32, (SIDE_ROWS, h), 1)
-    left = jnp.full((SIDE_ROWS, h), trace, F32)
-    line = jnp.zeros((SIDE_ROWS, h), F32)
+    return jnp.sum(jnp.where(row == col, diag - 0.25 * sign, 0.0) + sign * rounded * rounded)
+
+
+def in_pieces(value, shape):
+    lane = lax.broadcasted_iota(jnp.int32, shape, 1)
+    left, line = jnp.broadcast_to(value, shape).astype(F32), jnp.zeros(shape, F32)
     for k in range(3):
         piece = left.astype(BF).astype(F32)
         line = jnp.where(lane == k, piece, line)
         left = left - piece
-    rows_ref[...] = line
-    rows_ref[:ASIDE] = diag[size - ASIDE :, :h]
-    rows_ref[ASIDE : ASIDE + 1] = diag[size - 1 :, h:]
-    side = rows_ref[...].astype(BF)
+    return line
+
+
+def side_kernel(branch_ref, diag_ref, side_ref, rows_ref):
+    size = diag_ref.shape[0]
+    h = size // 2
+    rows_ref[...] = in_pieces(diagonal_trace(diag_ref[...], sign_of(branch_ref, 1)), rows_ref.shape)
+    rows_ref[:ASIDE] = diag_ref[size - ASIDE :, :h]
+    rows_ref[ASIDE : ASIDE + 1] = diag_ref[size - 1 :, h:]
+    side_ref[0] = rows_ref[...].astype(BF)
+
+
+def second_kernel(
+    cluster, branch_ref, cols_ref, x_ref, gathered_ref, own_ref, crossed_ref, new_ref, side_ref
+):
+    tiles, size = x_ref.shape[:2]
+    h = size // 2
+    sign = sign_of(branch_ref, 0)
+    grids = index_grids(h)
+    x0 = x_ref[0]
+    at = lax.broadcasted_iota(jnp.int32, (SIDE_ROWS, h), 0)
+    norms = jnp.zeros((SIDE_ROWS, h), F32)
+    for slot in range(1, tiles):
+        tile = x_ref[slot]
+        column = cols_ref[0, slot]
+        partner = holder_of(column, cluster)
+        rows = gathered_ref[partner, :size].astype(F32)
+        c_last = gathered_ref[partner, 2 * size - ASIDE :].astype(F32)
+        product = nn(tile, unfolded(rows[:h], rows[h:], c_last, grids))
+        new = tile.astype(F32) + sign * (nn(x0, tile) + product)
+        new_ref[slot - 1] = new
+        squares = new.astype(BF).astype(F32)
+        squares = squares * squares
+        main = squares[:h, :h] + squares[h:, h:]
+        even = 0.5 * (main + main.T) + (squares[:h, h:] + squares[h:, :h].T)
+        norms = jnp.where(at == NORMS + lax.rem(column, cluster // 2), jnp.sum(even, axis=0, keepdims=True), norms)
+    norms = jnp.sum(norms, axis=1, keepdims=True)
+    crossed, own = crossed_ref[0].astype(F32), own_ref[0].astype(F32)
+    pair = jnp.sum(jnp.where(at == NORMS - 1, crossed, 0.0)) + jnp.sum(jnp.where(at == NORMS - 1, own, 0.0))
+    side = jnp.where(at == NORMS - 1, in_pieces(pair, crossed.shape), crossed)
+    side = jnp.where(at >= NORMS, in_pieces(norms, crossed.shape), side).astype(BF)
     for slot in range(side_ref.shape[0]):
         side_ref[slot] = side
 
@@ -122,10 +144,17 @@
     tiles, size = out_ref.shape[:2]
     h = size // 2
     stores = [pltpu.make_async_copy(out_ref.at[s], out_hbm.at[s], store_sems.at[s]) for s in range(tiles)]
-    lines = jnp.zeros((SIDE_ROWS, h), F32)
-    for member in range(cluster):
-        lines += side_ref[member].astype(F32)
-    occupation_ref[0] = jnp.sum(lines[ASIDE + 1 : ASIDE + 2]) / (cluster * size) + 0.5
+    half = side_ref.shape[0]
+    read = [side_ref[member].astype(F32) for member in range(half)]
+    pairs = [read[member] + read[member + half // 2] for member in range(half // 2)]
+    diagonal = jnp.sum(sum(pairs)[NORMS - 1 : NORMS])
+    lane = lax.broadcasted_iota(jnp.int32, (half, h), 1)
+    norms = jnp.zeros((half, h), F32)
+    for member in range(half):
+        norms = jnp.where(lane == member, jnp.sum(read[member][NORMS:], axis=1, keepdims=True), norms)
+    norms = jnp.concatenate([norms, jnp.zeros((h - half, h), F32)], axis=0)
+    trace = diagonal + sign_of(branch_ref, 1) * jnp.sum(norms + norms.T)
+    occupation_ref[0] = trace / (cluster * size) + 0.5
     stores.append(pltpu.make_async_copy(occupation_ref, occupation_hbm, occupation_sem))
     stores[tiles].start()
     sign = sign_of(branch_ref, 1)
@@ -138,10 +167,11 @@
         r = new.astype(BF)
         total += nt(r, r)
         column = cols_ref[0, slot]
-        side = side_ref[lax.rem(column, cluster)].astype(F32)
-        rows = gathered_ref[holder_of(column, cluster), size : 2 * size - ASIDE].astype(F32)
+        holder = holder_of(column, cluster)
+        side = side_ref[holder].astype(F32)
+        rows = gathered_ref[holder, size : 2 * size - ASIDE].astype(F32)
         below = jnp.concatenate([rows[h:], side[:ASIDE]], axis=0)
-        product = symmetric_product(r, rows[:h], below, side[ASIDE : ASIDE + 1], grids)
+        product = nn(r, unfolded(rows[:h], below, side[ASIDE : ASIDE + 1], grids)).astype(BF).astype(F32)
         out_ref[slot] = new + sign * (nn(r0, r) + product)
         stores[slot].start()
     out_ref[0] = diag + sign * (total - quarter_identity(size))
@@ -184,16 +214,20 @@
         "first",
     )
     crossed = lax.ppermute(sent, "col", across)
+    (side,) = call(
+        side_kernel, (S, V), [((1, SIDE_ROWS, h), BF, V)], [pltpu.VMEM((SIDE_ROWS, h), F32)], (branch, diag), "side"
+    )
+    crossed_side = lax.ppermute(side, "col", across)
     gathered = lax.all_gather(crossed, "col", axis=0, tiled=True, axis_index_groups=halves)
-    new, side = call(
+    new, sides = call(
         lambda *refs: second_kernel(cluster, *refs),
-        (S, S, V, V, V),
-        [(fewer, F32, V), ((cluster, SIDE_ROWS, h), BF, V)],
-        [pltpu.VMEM((SIDE_ROWS, h), F32)],
-        (branch, columns, x, diag, gathered),
+        (S, S, V, V, V, V),
+        [(fewer, F32, V), ((cluster // 2, SIDE_ROWS, h), BF, V)],
+        [],
+        (branch, columns, x, gathered, side, crossed_side),
         "second",
     )
-    sides = lax.all_to_all(side, "col", 0, 0, tiled=True)
+    sides = lax.all_to_all(sides, "col", 0, 0, tiled=True, axis_index_groups=halves)
     out, occupation = call(
         lambda *refs: third_kernel(cluster, *refs),
         (S, S, V, V, V, V),

time: 60.7 us -> 56 us (0.923)
  blocking collectives: 34.2 us -> 28.6 us
  waiting for transfers between devices: 2.39 us -> 0.01 us
  starting transfers between devices: 16.9 us -> 18.9 us
  local copies, waits for them, and re-layouts: 0.01 us -> 0.67 us
    all_to_all x1, blocking collectives: 14.1 us -> 9.36 us  [shards(): lax.all_to_all(sides, 'col', 0, 0, tiled=True, axis_index_groups=halves)]
    ppermute x1, waiting for transfers between devices: 2.39 us -> 0.01 us  [shards(): crossed = lax.ppermute(sent, 'col', across)]
    ppermute x0 -> x1, starting transfers between devices: none -> 1.92 us  [shards(): crossed_side = lax.ppermute(side, 'col', across)]
    all_gather x1, blocking collectives: 20.1 us -> 19.3 us  [shards(): lax.all_gather(crossed, 'col', axis=0, tiled=True, axis_index_groups=halves)]
    unnamed x6 -> x8, local copies, waits for them, and re-layouts: 0.01 us -> 0.67 us
    pallas_call x3 -> x4, Pallas kernels: 6.31 us -> 6.88 us  [call(): pl.pallas_call(kernel, out_shape=[jax.ShapeDtypeStruct(shape, dtype) for...]
  transfers between devices with their start and end apart: 1 -> 2, of which waited for: 1 -> 0; matrix products, arithmetic and copies ran while one was open for 0% -> 0% of each run, Pallas kernels for 0% -> 1%
where the time goes in v5:
time: 56 us; the launch traced here: 55.7 us
  blocking collectives  28.6 us (51%)
  starting transfers between devices  18.9 us (34%)
  Pallas kernels  6.88 us (12%)
  between operations  0.71 us (1%)
  local copies, waits for them, and re-layouts  0.67 us (1%)
    all_gather x1, blocking collectives, shards(): lax.all_gather(crossed, 'col', axis=0, tiled=True, axis_index_groups=halves)  19.3 us
    ppermute x1, starting transfers between devices, shards(): crossed = lax.ppermute(sent, 'col', across)  16.9 us
    all_to_all x1, blocking collectives, shards(): lax.all_to_all(sides, 'col', 0, 0, tiled=True, axis_index_groups=halves)  9.36 us
    pallas_call x4, Pallas kernels, call(): pl.pallas_call(kernel, out_shape=[jax.ShapeDtypeStruct(shape, dtype) for...  6.88 us
    ppermute x1, starting transfers between devices, shards(): crossed_side = lax.ppermute(side, 'col', across)  1.92 us
  transfers between devices with their start and end apart: 2, of which 0 were waited for; matrix products, arithmetic and copies ran while one was open for 0% of the time, Pallas kernels for 1%

profile of v5, /device:TPU:1, one launch (start us, length us, event | category | flops | bytes accessed | tf_op | source)
XLA Modules:
  0.0 55.7 jit_solution(16075705840852055006)
XLA Ops:
  0.6 0.0 copy-start.2
  0.6 0.0 copy-start
  0.7 0.0 copy-start.3
  0.7 2.0 %first.1 = (bf16[1,505,128]{2,1,0:T(8,128)(2,1)S(1)}, f32[256,256]{1,0:T(8,128)S(1)}) custom-call(s32[1,2]{1,0:T(1,128)} %refs_0_.3, bf16[8,256,256]{2,1,0:T(8,128)(2,1)} %bitcast.2), custom_call_target="tpu_custom_call" | custom-call | tf_op jit(solution)/shard_map/first/pallas_call | solution.py:187
  2.6 16.9 %collective-permute-start = (bf16[1,505,128]{2,1,0:T(8,128)(2,1)S(1)}, bf16[1,505,128]{2,1,0:T(8,128)(2,1)S(1)}, u32[]{:S(2)}, u32[]{:S(2)}) collective-permute-start(bf16[1,505,128]{2,1,0:T(8,128)(2,1)S(1)} %get-tuple-element.9), channel_id=1, source_target_pairs={{0,12},{1,13},{2,14},{3,15},{4,8},{5,9},{6,10},{7,11},{8,4},{9,5},... | collective-permute-start | bytes 387848 | tf_op jit(solution)/shard_map/ppermute | solution.py:216
  19.6 0.0 copy-start.1
  19.6 0.6 %copy-done.1 = s32[1,2]{1,0:T(1,128)S(1)} copy-done((s32[1,2]{1,0:T(1,128)S(1)}, s32[1,2]{1,0:T(1,128)}, u32[]{:S(2)}) %copy-start.1) | copy-done | bytes 32
  20.3 0.8 %side.1.refs_4_ = bf16[1,24,128]{2,1,0:T(8,128)(2,1)S(1)} custom-call(s32[1,2]{1,0:T(1,128)S(1)} %copy-done.1, f32[256,256]{1,0:T(8,128)S(1)} %get-tuple-element.8.diag_ref.refs_2_), custom_call_target="tpu_custom_call" | custom-call | tf_op jit(solution)/shard_map/side/pallas_call | solution.py:187
  21.0 1.9 %collective-permute-start.1 = (bf16[1,24,128]{2,1,0:T(8,128)(2,1)S(1)}, bf16[1,24,128]{2,1,0:T(8,128)(2,1)S(1)}, u32[]{:S(2)}, u32[]{:S(2)}) collective-permute-start(bf16[1,24,128]{2,1,0:T(8,128)(2,1)S(1)} %side.1.refs_4_), channel_id=1, source_target_pairs={{0,12},{1,13},{2,14},{3,15},{4,8},{5,9},{6,10},{7,11},{8,4},{9,5},... | collective-permute-start | bytes 18440 | tf_op jit(solution)/shard_map/ppermute | solution.py:220
  22.9 0.0 collective-permute-done
  23.0 19.3 %all_gather.3.refs_3_.refs_4_ = bf16[8,505,128]{2,1,0:T(8,128)(2,1)S(1)} all-gather(bf16[1,505,128]{2,1,0:T(8,128)(2,1)S(1)} %collective-permute-done), channel_id=1, replica_groups={{0,1,2,3,4,5,6,7},{8,9,10,11,12,13,14,15},{16,17,18,19,20,21,22,23},{24..., dimensions={0}, use_global_device_ids=true | all-gather | bytes 1163520 | tf_op jit(solution)/shard_map/all_gather | solution.py:221
  42.2 0.0 collective-permute-done.1.refs_5_
  42.2 0.0 copy-done.2
  42.2 0.0 copy-done
  42.2 0.0 copy-done.3
  42.3 1.6 %second.1 = (f32[7,256,256]{2,1,0:T(8,128)S(1)}, bf16[8,24,128]{2,1,0:T(8,128)(2,1)S(1)}) custom-call(s32[1,2]{1,0:T(1,128)S(1)} %copy-done.2, s32[1,8]{1,0:T(1,128)S(1)} %copy-done.3, bf16[8,256,256]{2,1,0:T(8,128)(2,1)S(1)} %bitcast.3, bf16[8,505,128]{2,1,0:T(8,128)(2,1)S(1)} %all_gather.3.refs_3_.refs_4_, bf16[1,24,128]{2,1,0:T(8,128)(2,1)S(1)} %side.1.refs_4_, ...), custom_call_target="tpu_custom_call" | custom-call | tf_op jit(solution)/shard_map/second/pallas_call | solution.py:187
  43.8 9.4 %all_to_all.5.refs_5_ = bf16[8,24,128]{2,1,0:T(8,128)(2,1)S(1)} all-to-all(bf16[8,24,128]{2,1,0:T(8,128)(2,1)S(1)} %get-tuple-element.11), channel_id=1, replica_groups={{0,1,2,3,4,5,6,7},{8,9,10,11,12,13,14,15},{16,17,18,19,20,21,22,23},{24..., dimensions={0} | all-to-all | bytes 98304 | tf_op jit(solution)/shard_map/all_to_all | solution.py:230
  53.2 2.5 %third.1 = (f32[8,256,256]{2,1,0:T(8,128)}, f32[1]{0:T(128)}) custom-call(s32[1,2]{1,0:T(1,128)S(1)} %copy-done.2, s32[1,8]{1,0:T(1,128)S(1)} %copy-done.3, f32[256,256]{1,0:T(8,128)S(1)} %get-tuple-element.8.diag_ref.refs_2_, f32[7,256,256]{2,1,0:T(8,128)S(1)} %get-tuple-element.10.refs_3_, bf16[8,505,128]{2,1,0:T(8,128)(2,1)S(1)} %all_gather.3.refs_3_.refs_4_, ...), custom_call_target="tpu_custom_call" | custom-call | tf_op jit(solution)/shard_map/third/pallas_call | solution.py:187
Async XLA Ops:
  0.6 41.6 %copy-start.2 = (s32[1,2]{1,0:T(1,128)S(1)}, s32[1,2]{1,0:T(1,128)}, u32[]{:S(2)}) copy-start(s32[1,2]{1,0:T(1,128)} %refs_0_.3) | copy-start | bytes 28
  0.6 41.6 %copy-start = (bf16[1,8,256,256]{3,2,1,0:T(8,128)(2,1)S(1)}, bf16[1,8,256,256]{3,2,1,0:T(8,128)(2,1)}, u32[]{:S(2)}) copy-start(bf16[1,8,256,256]{3,2,1,0:T(8,128)(2,1)} %param.3) | copy-start | bytes 3145732
  0.7 41.6 %copy-start.3 = (s32[1,8]{1,0:T(1,128)S(1)}, s32[1,8]{1,0:T(1,128)}, u32[]{:S(2)}) copy-start(s32[1,8]{1,0:T(1,128)} %refs_1_.3) | copy-start | bytes 100
  2.6 20.3 %collective-permute-start = (bf16[1,505,128]{2,1,0:T(8,128)(2,1)S(1)}, bf16[1,505,128]{2,1,0:T(8,128)(2,1)S(1)}, u32[]{:S(2)}, u32[]{:S(2)}) collective-permute-start(bf16[1,505,128]{2,1,0:T(8,128)(2,1)S(1)} %get-tuple-element.9), channel_id=1, source_target_pairs={{0,12},{1,13},{2,14},{3,15},{4,8},{5,9},{6,10},{7,11},{8,4},{9,5},... | collective-permute-start | bytes 387848 | tf_op jit(solution)/shard_map/ppermute | solution.py:216
  19.6 0.7 %copy-start.1 = (s32[1,2]{1,0:T(1,128)S(1)}, s32[1,2]{1,0:T(1,128)}, u32[]{:S(2)}) copy-start(s32[1,2]{1,0:T(1,128)} %refs_0_.3) | copy-start | bytes 28
  21.0 21.2 %collective-permute-start.1 = (bf16[1,24,128]{2,1,0:T(8,128)(2,1)S(1)}, bf16[1,24,128]{2,1,0:T(8,128)(2,1)S(1)}, u32[]{:S(2)}, u32[]{:S(2)}) collective-permute-start(bf16[1,24,128]{2,1,0:T(8,128)(2,1)S(1)} %side.1.refs_4_), channel_id=1, source_target_pairs={{0,12},{1,13},{2,14},{3,15},{4,8},{5,9},{6,10},{7,11},{8,4},{9,5},... | collective-permute-start | bytes 18440 | tf_op jit(solution)/shard_map/ppermute | solution.py:220

commit v6 on v5

--- a/solution.py
+++ b/solution.py
@@ -44,7 +44,7 @@
     return jnp.concatenate([above, under], axis=0).astype(BF)
 
 
-SIDE_ROWS, ASIDE, NORMS = 24, 8, 16
+SIDE_ROWS, ASIDE, PIECES = 16, 8, 9
 
 
 def holder_of(column, cluster):
@@ -113,7 +113,8 @@
     grids = index_grids(h)
     x0 = x_ref[0]
     at = lax.broadcasted_iota(jnp.int32, (SIDE_ROWS, h), 0)
-    norms = jnp.zeros((SIDE_ROWS, h), F32)
+    lane = lax.broadcasted_iota(jnp.int32, (SIDE_ROWS, h), 1)
+    sums = jnp.zeros((SIDE_ROWS, h), F32)
     for slot in range(1, tiles):
         tile = x_ref[slot]
         column = cols_ref[0, slot]
@@ -127,12 +128,16 @@
         squares = squares * squares
         main = squares[:h, :h] + squares[h:, h:]
         even = 0.5 * (main + main.T) + (squares[:h, h:] + squares[h:, :h].T)
-        norms = jnp.where(at == NORMS + lax.rem(column, cluster // 2), jnp.sum(even, axis=0, keepdims=True), norms)
-    norms = jnp.sum(norms, axis=1, keepdims=True)
+        norm = jnp.sum(jnp.sum(even, axis=0, keepdims=True), axis=1, keepdims=True)
+        sums = jnp.where(lane == lax.rem(column, cluster // 2), norm, sums)
     crossed, own = crossed_ref[0].astype(F32), own_ref[0].astype(F32)
-    pair = jnp.sum(jnp.where(at == NORMS - 1, crossed, 0.0)) + jnp.sum(jnp.where(at == NORMS - 1, own, 0.0))
-    side = jnp.where(at == NORMS - 1, in_pieces(pair, crossed.shape), crossed)
-    side = jnp.where(at >= NORMS, in_pieces(norms, crossed.shape), side).astype(BF)
+    pair = jnp.sum(jnp.where(at == PIECES, crossed, 0.0)) + jnp.sum(jnp.where(at == PIECES, own, 0.0))
+    left, side = jnp.where(lane == cluster // 2, pair, sums), crossed
+    for k in range(3):
+        piece = left.astype(BF).astype(F32)
+        side = jnp.where(at == PIECES + k, piece, side)
+        left = left - piece
+    side = side.astype(BF)
     for slot in range(side_ref.shape[0]):
         side_ref[slot] = side
 
@@ -146,12 +151,15 @@
     stores = [pltpu.make_async_copy(out_ref.at[s], out_hbm.at[s], store_sems.at[s]) for s in range(tiles)]
     half = side_ref.shape[0]
     read = [side_ref[member].astype(F32) for member in range(half)]
-    pairs = [read[member] + read[member + half // 2] for member in range(half // 2)]
-    diagonal = jnp.sum(sum(pairs)[NORMS - 1 : NORMS])
+    lines = [r[PIECES : PIECES + 1] + r[PIECES + 1 : PIECES + 2] + r[PIECES + 2 : PIECES + 3] for r in read]
+    pairs = sum(lines[member] + lines[member + half // 2] for member in range(half // 2))
     lane = lax.broadcasted_iota(jnp.int32, (half, h), 1)
+    diagonal = jnp.sum(jnp.where(lane[:1] == half, pairs, 0.0))
+    at = lax.broadcasted_iota(jnp.int32, (half, h), 0)
     norms = jnp.zeros((half, h), F32)
     for member in range(half):
-        norms = jnp.where(lane == member, jnp.sum(read[member][NORMS:], axis=1, keepdims=True), norms)
+        norms = jnp.where(at == member, lines[member], norms)
+    norms = jnp.where(lane < half, norms, 0.0)
     norms = jnp.concatenate([norms, jnp.zeros((h - half, h), F32)], axis=0)
     trace = diagonal + sign_of(branch_ref, 1) * jnp.sum(norms + norms.T)
     occupation_ref[0] = trace / (cluster * size) + 0.5

time: 56 us -> 56 us (level)
  no operation moved by 1% of the time
where the time goes in v6:
time: 56 us; the launch traced here: 55.7 us
  blocking collectives  28.5 us (51%)
  starting transfers between devices  18.9 us (34%)
  Pallas kernels  6.95 us (12%)
  between operations  0.71 us (1%)
  local copies, waits for them, and re-layouts  0.67 us (1%)
    all_gather x1, blocking collectives, shards(): lax.all_gather(crossed, 'col', axis=0, tiled=True, axis_index_groups=halves)  19.1 us
    ppermute x1, starting transfers between devices, shards(): crossed = lax.ppermute(sent, 'col', across)  16.9 us
    all_to_all x1, blocking collectives, shards(): lax.all_to_all(sides, 'col', 0, 0, tiled=True, axis_index_groups=halves)  9.41 us
    pallas_call x4, Pallas kernels, call(): pl.pallas_call(kernel, out_shape=[jax.ShapeDtypeStruct(shape, dtype) for...  6.95 us
    ppermute x1, starting transfers between devices, shards(): crossed_side = lax.ppermute(side, 'col', across)  1.92 us
  transfers between devices with their start and end apart: 2, of which 0 were waited for; matrix products, arithmetic and copies ran while one was open for 0% of the time, Pallas kernels for 1%

profile of v6, /device:TPU:1, one launch (start us, length us, event | category | flops | bytes accessed | tf_op | source)
XLA Modules:
  0.0 55.7 jit_solution(16981760890350355113)
XLA Ops:
  0.6 0.0 copy-start.2
  0.6 0.0 copy-start
  0.7 0.0 copy-start.3
  0.7 2.0 %first.1 = (bf16[1,505,128]{2,1,0:T(8,128)(2,1)S(1)}, f32[256,256]{1,0:T(8,128)S(1)}) custom-call(s32[1,2]{1,0:T(1,128)} %refs_0_.3, bf16[8,256,256]{2,1,0:T(8,128)(2,1)} %bitcast.2), custom_call_target="tpu_custom_call" | custom-call | tf_op jit(solution)/shard_map/first/pallas_call | solution.py:195
  2.6 16.9 %collective-permute-start = (bf16[1,505,128]{2,1,0:T(8,128)(2,1)S(1)}, bf16[1,505,128]{2,1,0:T(8,128)(2,1)S(1)}, u32[]{:S(2)}, u32[]{:S(2)}) collective-permute-start(bf16[1,505,128]{2,1,0:T(8,128)(2,1)S(1)} %get-tuple-element.9), channel_id=1, source_target_pairs={{0,12},{1,13},{2,14},{3,15},{4,8},{5,9},{6,10},{7,11},{8,4},{9,5},... | collective-permute-start | bytes 387848 | tf_op jit(solution)/shard_map/ppermute | solution.py:224
  19.6 0.0 copy-start.1
  19.6 0.6 %copy-done.1 = s32[1,2]{1,0:T(1,128)S(1)} copy-done((s32[1,2]{1,0:T(1,128)S(1)}, s32[1,2]{1,0:T(1,128)}, u32[]{:S(2)}) %copy-start.1) | copy-done | bytes 32
  20.3 0.8 %side.1.refs_4_ = bf16[1,16,128]{2,1,0:T(8,128)(2,1)S(1)} custom-call(s32[1,2]{1,0:T(1,128)S(1)} %copy-done.1, f32[256,256]{1,0:T(8,128)S(1)} %get-tuple-element.8.diag_ref.refs_2_), custom_call_target="tpu_custom_call" | custom-call | tf_op jit(solution)/shard_map/side/pallas_call | solution.py:195
  21.0 1.9 %collective-permute-start.1 = (bf16[1,16,128]{2,1,0:T(8,128)(2,1)S(1)}, bf16[1,16,128]{2,1,0:T(8,128)(2,1)S(1)}, u32[]{:S(2)}, u32[]{:S(2)}) collective-permute-start(bf16[1,16,128]{2,1,0:T(8,128)(2,1)S(1)} %side.1.refs_4_), channel_id=1, source_target_pairs={{0,12},{1,13},{2,14},{3,15},{4,8},{5,9},{6,10},{7,11},{8,4},{9,5},... | collective-permute-start | bytes 12296 | tf_op jit(solution)/shard_map/ppermute | solution.py:228
  22.9 0.0 collective-permute-done
  23.0 19.1 %all_gather.3.refs_3_.refs_4_ = bf16[8,505,128]{2,1,0:T(8,128)(2,1)S(1)} all-gather(bf16[1,505,128]{2,1,0:T(8,128)(2,1)S(1)} %collective-permute-done), channel_id=1, replica_groups={{0,1,2,3,4,5,6,7},{8,9,10,11,12,13,14,15},{16,17,18,19,20,21,22,23},{24..., dimensions={0}, use_global_device_ids=true | all-gather | bytes 1163520 | tf_op jit(solution)/shard_map/all_gather | solution.py:229
  42.1 0.0 collective-permute-done.1.refs_5_
  42.1 0.0 copy-done.2
  42.1 0.0 copy-done
  42.1 0.0 copy-done.3
  42.1 1.7 %second.1 = (f32[7,256,256]{2,1,0:T(8,128)S(1)}, bf16[8,16,128]{2,1,0:T(8,128)(2,1)S(1)}) custom-call(s32[1,2]{1,0:T(1,128)S(1)} %copy-done.2, s32[1,8]{1,0:T(1,128)S(1)} %copy-done.3, bf16[8,256,256]{2,1,0:T(8,128)(2,1)S(1)} %bitcast.3, bf16[8,505,128]{2,1,0:T(8,128)(2,1)S(1)} %all_gather.3.refs_3_.refs_4_, bf16[1,16,128]{2,1,0:T(8,128)(2,1)S(1)} %side.1.refs_4_, ...), custom_call_target="tpu_custom_call" | custom-call | tf_op jit(solution)/shard_map/second/pallas_call | solution.py:195
  43.8 9.4 %all_to_all.5.refs_5_ = bf16[8,16,128]{2,1,0:T(8,128)(2,1)S(1)} all-to-all(bf16[8,16,128]{2,1,0:T(8,128)(2,1)S(1)} %get-tuple-element.11), channel_id=1, replica_groups={{0,1,2,3,4,5,6,7},{8,9,10,11,12,13,14,15},{16,17,18,19,20,21,22,23},{24..., dimensions={0} | all-to-all | bytes 65536 | tf_op jit(solution)/shard_map/all_to_all | solution.py:238
  53.2 2.5 %third.1 = (f32[8,256,256]{2,1,0:T(8,128)}, f32[1]{0:T(128)}) custom-call(s32[1,2]{1,0:T(1,128)S(1)} %copy-done.2, s32[1,8]{1,0:T(1,128)S(1)} %copy-done.3, f32[256,256]{1,0:T(8,128)S(1)} %get-tuple-element.8.diag_ref.refs_2_, f32[7,256,256]{2,1,0:T(8,128)S(1)} %get-tuple-element.10.refs_3_, bf16[8,505,128]{2,1,0:T(8,128)(2,1)S(1)} %all_gather.3.refs_3_.refs_4_, ...), custom_call_target="tpu_custom_call" | custom-call | tf_op jit(solution)/shard_map/third/pallas_call | solution.py:195
Async XLA Ops:
  0.6 41.5 %copy-start.2 = (s32[1,2]{1,0:T(1,128)S(1)}, s32[1,2]{1,0:T(1,128)}, u32[]{:S(2)}) copy-start(s32[1,2]{1,0:T(1,128)} %refs_0_.3) | copy-start | bytes 28
  0.6 41.4 %copy-start = (bf16[1,8,256,256]{3,2,1,0:T(8,128)(2,1)S(1)}, bf16[1,8,256,256]{3,2,1,0:T(8,128)(2,1)}, u32[]{:S(2)}) copy-start(bf16[1,8,256,256]{3,2,1,0:T(8,128)(2,1)} %param.3) | copy-start | bytes 3145732
  0.7 41.4 %copy-start.3 = (s32[1,8]{1,0:T(1,128)S(1)}, s32[1,8]{1,0:T(1,128)}, u32[]{:S(2)}) copy-start(s32[1,8]{1,0:T(1,128)} %refs_1_.3) | copy-start | bytes 100
  2.6 20.3 %collective-permute-start = (bf16[1,505,128]{2,1,0:T(8,128)(2,1)S(1)}, bf16[1,505,128]{2,1,0:T(8,128)(2,1)S(1)}, u32[]{:S(2)}, u32[]{:S(2)}) collective-permute-start(bf16[1,505,128]{2,1,0:T(8,128)(2,1)S(1)} %get-tuple-element.9), channel_id=1, source_target_pairs={{0,12},{1,13},{2,14},{3,15},{4,8},{5,9},{6,10},{7,11},{8,4},{9,5},... | collective-permute-start | bytes 387848 | tf_op jit(solution)/shard_map/ppermute | solution.py:224
  19.6 0.7 %copy-start.1 = (s32[1,2]{1,0:T(1,128)S(1)}, s32[1,2]{1,0:T(1,128)}, u32[]{:S(2)}) copy-start(s32[1,2]{1,0:T(1,128)} %refs_0_.3) | copy-start | bytes 28
  21.0 21.1 %collective-permute-start.1 = (bf16[1,16,128]{2,1,0:T(8,128)(2,1)S(1)}, bf16[1,16,128]{2,1,0:T(8,128)(2,1)S(1)}, u32[]{:S(2)}, u32[]{:S(2)}) collective-permute-start(bf16[1,16,128]{2,1,0:T(8,128)(2,1)S(1)} %side.1.refs_4_), channel_id=1, source_target_pairs={{0,12},{1,13},{2,14},{3,15},{4,8},{5,9},{6,10},{7,11},{8,4},{9,5},... | collective-permute-start | bytes 12296 | tf_op jit(solution)/shard_map/ppermute | solution.py:228
